TPU v7x, 256 devices: a whole 4x4x8 slice. The times are simulated.
256 devices in a mesh: rows: 64 (over z, x, core), feat: 4 (over y).
Axes of the slice: x: 4, y: 4, z: 8, core: 2. Of those that a mesh axis runs over, the one named last changes fastest.
Arguments:
- features: float32 [131072, 1024], P('rows', 'feat')
- norm_gain: float32 [1024], P('feat'), may hold values from 0.1 to 1.9
- row_counts: int32 [64, 16], P('rows'), may hold values from 1 to 64, 128 in all within a row
- tile_cols: int32 [8192], P('rows'), may hold values from 0 to 1023, as said below
- tile_values: float32 [8192, 128, 128], P('rows'), may hold values from -0.1875 to 0.1875
Outputs:
- normed: float32 [131072, 1024], P('rows', 'feat')
Inputs may be any that keep to these rules, and one draw needn't show every extreme that they name: `tile_cols`: node n lies in stripe n // 2048. There are exactly 3 heavy stripes; every device's tiles reference every block of every heavy stripe and every block of its own stripe. Every other block that a device's tiles reference is referenced by one of its tiles only, lies in no heavy stripe, and no two such blocks of one device lie in the same stripe; each device has exactly 45 such blocks. `row_counts`: each device's counts sum to 128.
All inputs are finite; a program needn't handle non-finite values.
Results may differ from a plain program's by a relative error of at most 0.0003.
Values sent between devices are 32-bit elements; how exact they have to be, the bound alone decides.
A program may use at most 128 MiB of HBM per device.

v0:
```python
import jax
import jax.numpy as jnp
from jax import lax
from jax.sharding import PartitionSpec as P

HEAVY = 3


def broadcast(block, axis, owner):
    block = jnp.where(lax.axis_index(axis) == owner, block, jnp.zeros_like(block))
    return lax.psum(block, axis)


def per_device(features, norm_gain, row_counts, tile_cols, tile_values):
    node_dev, feat_dev = features.shape
    block_rows = tile_values.shape[1]
    blocks_dev = node_dev // block_rows
    tile_total = tile_values.shape[0]
    heavy_count = HEAVY
    devices = lax.axis_size("rows")
    my_index = lax.axis_index("rows")
    activated = jnp.maximum(features, 0.0)
    act_blocks = activated.reshape(blocks_dev, block_rows, feat_dev)
    owner_dev = tile_cols // blocks_dev
    local_block = tile_cols % blocks_dev
    is_own = owner_dev == my_index
    peer_ids = jnp.arange(devices, dtype=jnp.int32)
    block_ids = jnp.arange(blocks_dev, dtype=jnp.int32)
    to_peer = (owner_dev[None, :] == peer_ids[:, None]) & jnp.logical_not(is_own)[None, :]
    block_hit = jnp.any(
        to_peer[:, None, :] & (local_block[None, None, :] == block_ids[None, :, None]), axis=2
    )
    seen_count = jnp.sum(block_hit.astype(jnp.int32), axis=1)
    local_mark = (seen_count >= 2).astype(jnp.int32)
    heavy_mark = lax.pmax(local_mark, "rows")
    heavy_rank = jnp.cumsum(heavy_mark, dtype=jnp.int32) - 1
    heavy_list = []
    for stripe in range(heavy_count):
        heavy_list.append(
            jnp.sum(jnp.where((heavy_mark > 0) & (heavy_rank == stripe), peer_ids, 0))
        )
    heavy_ids = jnp.stack(heavy_list)
    stripes = []
    for stripe in range(heavy_count):
        stripes.append(broadcast(activated, "rows", heavy_ids[stripe]))
    heavy_blocks = jnp.stack(stripes).reshape(heavy_count * blocks_dev, block_rows, feat_dev)
    match_heavy = owner_dev[:, None] == heavy_ids[None, :]
    is_heavy = jnp.any(match_heavy, axis=1) & jnp.logical_not(is_own)
    stripe_ids = jnp.arange(heavy_count, dtype=jnp.int32)
    heavy_slot = (
        jnp.sum(match_heavy.astype(jnp.int32) * stripe_ids[None, :], axis=1) * blocks_dev
        + local_block
    )
    is_light = jnp.logical_not(is_own | is_heavy)
    to_owner = is_light[None, :] & (owner_dev[None, :] == peer_ids[:, None])
    wanted = jnp.max(jnp.where(to_owner, local_block[None, :], -1), axis=1)
    requested = lax.all_to_all(
        wanted.reshape(devices, 1), "rows", split_axis=0, concat_axis=0, tiled=True
    )[:, 0]
    request_valid = requested >= 0
    served = act_blocks[jnp.maximum(requested, 0)]
    outgoing = jnp.where(request_valid[:, None, None], served, 0.0)
    tile_counts = row_counts[0]
    row_ends = jnp.cumsum(tile_counts, dtype=jnp.int32)
    tile_index = jnp.arange(tile_total, dtype=jnp.int32)
    tile_row = jnp.sum((row_ends[None, :] <= tile_index[:, None]).astype(jnp.int32), axis=1)
    row_ids = jnp.arange(blocks_dev, dtype=jnp.int32)
    arrived = lax.all_to_all(outgoing, "rows", split_axis=0, concat_axis=0, tiled=True)
    panel = jnp.concatenate([heavy_blocks, arrived, act_blocks], axis=0)
    panel_slot = jnp.where(
        is_own,
        heavy_count * blocks_dev + devices + local_block,
        jnp.where(is_heavy, heavy_slot, heavy_count * blocks_dev + owner_dev),
    )
    picked = panel[panel_slot]
    products = jnp.einsum("tij,tjf->tif", tile_values, picked, precision=lax.Precision.HIGHEST)
    onehot = (tile_row[None, :] == row_ids[:, None]).astype(jnp.float32)
    aggregate = jnp.dot(
        onehot,
        products.reshape(tile_total, block_rows * feat_dev),
        precision=lax.Precision.HIGHEST,
        preferred_element_type=jnp.float32,
    )
    aggregate = aggregate.reshape(node_dev, feat_dev)
    square_sum = lax.psum(jnp.sum(aggregate * aggregate, axis=1), "feat")
    mean_square = square_sum / (feat_dev * lax.axis_size("feat"))
    return aggregate * norm_gain[None, :] * lax.rsqrt(mean_square + 1e-05)[:, None]


def solution(mesh):
    placed = (P("rows", "feat"), P("feat"), P("rows", None), P("rows"), P("rows", None, None))
    return jax.shard_map(
        per_device, mesh=mesh, in_specs=placed, out_specs=P("rows", "feat"), check_vma=False
    )
```

profile of v0, /device:TPU:1, one launch (start us, length us, event | category | flops | bytes accessed | tf_op | source)
XLA Modules:
  0.0 500.7 jit_solution(3899709780704313488)
XLA Ops:
  7.2 0.7 fusion.8
  7.9 1.2 and_reduce_fusion
  9.2 20.5 %pmax.7 = s32[64]{0:T(128)S(1)} all-reduce(s32[64]{0:T(128)S(1)} %compare_convert_fusion), channel_id=1, replica_groups=mesh['rows'=64,'feat'=4] {'rows'}, use_global_device_ids=true, to_apply=%region_4.5 | all-reduce | flops 64 | bytes 512 | tf_op jit(solution)/shard_map/pmax | solution.py:35
  30.0 0.7 fusion.5
  30.8 2.0 pad_add_fusion
  33.0 0.7 copy.31
  33.7 8.8 %all-to-all-start = ((s32[64,1,1]{2,1,0:T(1,128)}), s32[64,1,1]{2,1,0:T(1,128)S(1)}, u32[]{:S(2)}, u32[]{:S(2)}) async-start(s32[64,1,1]{2,1,0:T(1,128)} %copy.31), calls=%async_computation | async-start | bytes 65536 | tf_op jit(solution)/shard_map/all_to_all | solution.py:57
  44.4 4.6 select_bitcast_fusion.2
  49.0 3.0 all-to-all-done
  52.0 1.2 maximum_reduce_fusion
  53.2 4.3 gather_fusion
  57.5 1.2 compare_reduce_fusion
  58.7 8.3 %broadcast_select_fusion = f32[64,128,256]{2,1,0:T(8,128)} fusion(f32[64,128,256]{2,1,0:T(8,128)} %gather_fusion, pred[64]{0:T(512)(128)(4,1)S(1)} %compare_reduce_fusion), kind=kLoop, calls=%fused_computation.5 | loop fusion | flops 2097152 | bytes 16777280 | tf_op jit(solution)/shard_map/jit(_where)/select_n | solution.py:62
  67.1 7.6 %all-to-all-start.1 = ((f32[64,128,256]{2,1,0:T(8,128)}), f32[64,128,256]{2,1,0:T(8,128)}, u32[]{:S(2)}, u32[]{:S(2)}) async-start(f32[64,128,256]{2,1,0:T(8,128)} %broadcast_select_fusion), calls=%async_computation.1 | async-start | bytes 16777216 | tf_op jit(solution)/shard_map/all_to_all | solution.py:68
  75.9 308.6 %all-reduce.3.cloned.1.call-done = (f32[1,2048,256]{2,1,0:T(8,128)}, f32[1,2048,256]{2,1,0:T(8,128)}, f32[1,2048,256]{2,1,0:T(8,128)}) async-done(((f32[1,2048,256]{2,1,0:T(8,128)}, f32[1,2048,256]{2,1,0:T(8,128)}, f32[1,2048,256]{2,1,0:T(8,128)}), (f32[1,2048,256]{2,1,0:T(8,128)}, f32[1,2048,256]{2,1,0:T(8,128)}, f32[1,2048,256]{2,1,0:T(8,128)})) %all-reduce.3.cloned.1.call-update) | async-done | bytes 6291472 | tf_op jit(solution)/shard_map/psum | solution.py:11
  384.5 6.0 %pad_maximum_fusion.1 = f32[3,2048,256]{2,1,0:T(8,128)} fusion(f32[1,2048,256]{2,1,0:T(8,128)} %get-tuple-element.11, f32[1,2048,256]{2,1,0:T(8,128)} %get-tuple-element.12, f32[1,2048,256]{2,1,0:T(8,128)} %get-tuple-element.13), kind=kLoop, calls=%fused_computation.4 | loop fusion | flops 3145728 | bytes 12582912 | tf_op jit(solution)/shard_map/stack | solution.py:46
  390.5 11.3 %pad_maximum_fusion = f32[128,128,256]{2,1,0:T(8,128)} fusion(f32[16,128,256]{2,1,0:T(8,128)S(1)} %bitcast.22, f32[64,128,256]{2,1,0:T(8,128)} %all-to-all-done.1, f32[48,128,256]{2,1,0:T(8,128)} %bitcast.23), kind=kLoop, calls=%fused_computation.2 | loop fusion | flops 8388608 | bytes 33554432 | tf_op jit(solution)/shard_map/concatenate | solution.py:69
  401.8 15.6 %gather_fusion.1 = f32[128,128,256]{2,1,0:T(8,128)} fusion(f32[128,128,256]{2,1,0:T(8,128)} %pad_maximum_fusion, s32[1024]{0:T(1024)S(1)} %pad_clamp_fusion), kind=kCustom, calls=%fused_computation.1 | custom fusion | bytes 33554944 | tf_op jit(solution)/shard_map/gather | solution.py:75
  417.5 34.4 %convolution_bitcast_fusion = f32[128,128,256]{1,2,0:T(8,128)} fusion(f32[128,128,256]{2,1,0:T(8,128)} %gather_fusion.1, f32[128,128,128]{2,1,0:T(8,128)} %param.9), kind=kOutput, calls=%fused_computation.3 | convolution fusion | flops 6442450944 | bytes 41943040 | tf_op jit(solution)/shard_map/tij,tjf->tif/dot_general | solution.py:76
  451.8 17.6 %copy.33 = f32[128,128,256]{0,2,1:T(8,128)} copy(f32[128,128,256]{1,2,0:T(8,128)} %convolution_bitcast_fusion) | data formatting | bytes 33554432 | tf_op jit(solution)/shard_map/tij,tjf->tif/dot_general | solution.py:76
  469.5 12.1 %fusion.2 = f32[16,32768]{1,0:T(8,128)} fusion(f32[128,32768]{0,1:T(8,128)} %bitcast.20, s32[128]{0:T(128)S(1)} %convert_reduce_fusion.1), kind=kOutput, calls=%fused_computation.28 | convolution fusion | flops 805308416 | bytes 18874880 | tf_op jit(solution)/shard_map/dot_general | solution.py:78
  481.6 1.7 reshape.152
  483.6 8.6 %psum.31 = f32[2048]{0:T(1024)S(1)} all-reduce(f32[2048]{0:T(1024)S(1)} %multiply_reduce_fusion), channel_id=1, replica_groups=mesh['rows'=64,'feat'=4] {'feat'}, use_global_device_ids=true, to_apply=%region_16.17 | all-reduce | flops 2048 | bytes 16384 | tf_op jit(solution)/shard_map/psum | solution.py:85
  492.2 1.7 multiply_multiply_fusion
  (31 shorter events, 2.9 us)
Async XLA Ops:
  33.7 18.3 %all-to-all-start = ((s32[64,1,1]{2,1,0:T(1,128)}), s32[64,1,1]{2,1,0:T(1,128)S(1)}, u32[]{:S(2)}, u32[]{:S(2)}) async-start(s32[64,1,1]{2,1,0:T(1,128)} %copy.31), calls=%async_computation | async-start | bytes 65536 | tf_op jit(solution)/shard_map/all_to_all | solution.py:57
  67.1 323.5 %all-to-all-start.1 = ((f32[64,128,256]{2,1,0:T(8,128)}), f32[64,128,256]{2,1,0:T(8,128)}, u32[]{:S(2)}, u32[]{:S(2)}) async-start(f32[64,128,256]{2,1,0:T(8,128)} %broadcast_select_fusion), calls=%async_computation.1 | async-start | bytes 16777216 | tf_op jit(solution)/shard_map/all_to_all | solution.py:68
  74.7 0.8 copy-start.2
  74.7 1.1 copy-start
  74.7 309.8 %all-reduce.3.cloned.1.call-start = ((), (), s32[]{:S(2)}) async-start(), calls=%async_computation.2 | async-start | bytes 12582912 | tf_op jit(solution)/shard_map/psum | solution.py:11
  481.6 10.7 %copy-start.1 = (f32[256]{0:T(256)S(1)}, f32[256]{0:T(256)}, u32[]{:S(2)}) copy-start(f32[256]{0:T(256)} %param.6) | copy-start | bytes 3076
Sparse Core Ops, SparseCore 0:
  79.4 305.0 all-reduce.2
where the time goes:
time: 504 us; the launch traced here: 501 us
  waiting for transfers between devices  312 us (62%)
  matrix products  46.5 us (9%)
  other arithmetic  40.7 us (8%)
  local copies, waits for them, and re-layouts  40.3 us (8%)
  blocking collectives  29.1 us (6%)
  starting transfers between devices  16.6 us (3%)
  between operations  15.5 us (3%)
    psum x1, waiting for transfers between devices, broadcast(): return lax.psum(block, axis)  309 us
    dot_general x1, matrix products, per_device(): jnp.einsum('tij,tjf->tif', tile_values, picked, precision=lax.Precision.H...  34.4 us
    pmax x1, blocking collectives, per_device(): heavy_mark = lax.pmax(local_mark, 'rows')  20.5 us
    dot_general x1, local copies, waits for them, and re-layouts, per_device(): jnp.einsum('tij,tjf->tif', tile_values, picked, precision=lax.Precision.H...  17.6 us
    gather x1, local copies, waits for them, and re-layouts, per_device(): picked = panel[panel_slot]  15.6 us
    dot_general x1, matrix products, per_device(): jnp.dot(onehot, products.reshape(tile_total, block_rows * feat_dev), prec...  12.1 us
    concatenate x1, other arithmetic, per_device(): panel = jnp.concatenate([heavy_blocks, arrived, act_blocks], axis=0)  11.3 us
    another operation x2, other arithmetic, per_device(): jnp.stack(stripes).reshape(heavy_count * blocks_dev, block_rows, feat_dev)  10.6 us
  transfers between devices with their start and end apart: 3, of which 2 were waited for; matrix products, arithmetic and copies ran while one was open for 2% of the time, Pallas kernels for 0%

commit v1 on v0

v1 whole, which is shorter than its diff:
```python
import functools

import jax
import jax.numpy as jnp
from jax import lax
from jax.experimental import pallas as pl
from jax.experimental.pallas import tpu as pltpu
from jax.sharding import PartitionSpec as P

HEAVY = 3
GROUP = 16
DEPTH = 16
CHUNK = 8


def tile_kernel(slot, row, tiles, arrived, heavy, own, out, abuf, xbuf, asem, xsem):
    total = tiles.shape[0]
    n_arr, n_heavy = arrived.shape[0], heavy.shape[0]

    def tile_copy(c):
        part = pl.ds(c * CHUNK, CHUNK)
        return pltpu.make_async_copy(tiles.at[part], abuf.at[part], asem.at[c])

    def fetch(t):
        s, b = slot[t], lax.rem(t, DEPTH)

        @pl.when(s < n_arr)
        def _():
            pltpu.make_async_copy(arrived.at[s], xbuf.at[b], xsem.at[b]).start()

        @pl.when((s >= n_arr) & (s < n_arr + n_heavy))
        def _():
            pltpu.make_async_copy(heavy.at[s - n_arr], xbuf.at[b], xsem.at[b]).start()

        @pl.when(s >= n_arr + n_heavy)
        def _():
            pltpu.make_async_copy(own.at[s - n_arr - n_heavy], xbuf.at[b], xsem.at[b]).start()

    for c in range(2):
        tile_copy(c).start()

    @pl.loop(0, DEPTH)
    def _(t):
        fetch(t)

    @pl.loop(2, total // CHUNK)
    def _(c):
        tile_copy(c).start()

    out[...] = jnp.zeros_like(out)

    @pl.loop(0, total)
    def _(t):
        b = lax.rem(t, DEPTH)

        @pl.when(lax.rem(t, CHUNK) == 0)
        def _():
            tile_copy(t // CHUNK).wait()

        pltpu.make_async_copy(arrived.at[0], xbuf.at[b], xsem.at[b]).wait()
        a = abuf[t]
        x = jnp.maximum(xbuf[b], 0.0)
        a_hi = a.astype(jnp.bfloat16)
        a_lo = (a - a_hi.astype(jnp.float32)).astype(jnp.bfloat16)
        x_hi = x.astype(jnp.bfloat16)
        x_lo = (x - x_hi.astype(jnp.float32)).astype(jnp.bfloat16)
        prod = jnp.dot(
            jnp.concatenate([a_hi, a_lo], axis=1),
            jnp.concatenate([x_hi, x_hi], axis=0),
            preferred_element_type=jnp.float32,
        ) + jnp.dot(a_hi, x_lo, preferred_element_type=jnp.float32)
        out[row[t]] += prod

        @pl.when(t + DEPTH < total)
        def _():
            fetch(t + DEPTH)


def tile_product(slot, row, tiles, arrived, heavy, own):
    blocks, side, feat = own.shape
    total = tiles.shape[0]
    smem = pl.BlockSpec(memory_space=pltpu.SMEM)
    anywhere = pl.BlockSpec(memory_space=pl.ANY)
    return pl.pallas_call(
        tile_kernel,
        out_shape=jax.ShapeDtypeStruct((blocks, side, feat), jnp.float32),
        in_specs=[smem, smem, anywhere, anywhere, anywhere, anywhere],
        out_specs=pl.BlockSpec(memory_space=pltpu.VMEM),
        scratch_shapes=[
            pltpu.VMEM(tiles.shape, jnp.float32),
            pltpu.VMEM((DEPTH, side, feat), jnp.float32),
            pltpu.SemaphoreType.DMA((total // CHUNK,)),
            pltpu.SemaphoreType.DMA((DEPTH,)),
        ],
        compiler_params=pltpu.CompilerParams(vmem_limit_bytes=40 << 20),
    )(slot, row, tiles, arrived, heavy, own)


def pick_kernel(which, source, out, sem):
    count = out.shape[0]

    @pl.loop(0, count)
    def _(i):
        pltpu.make_async_copy(source.at[which[i]], out.at[i], sem.at[i]).start()

    @pl.loop(0, count)
    def _(i):
        pltpu.make_async_copy(source.at[which[i]], out.at[i], sem.at[i]).wait()


def pick(which, source):
    count = which.shape[0]
    anywhere = pl.BlockSpec(memory_space=pl.ANY)
    return pl.pallas_call(
        pick_kernel,
        out_shape=jax.ShapeDtypeStruct((count,) + source.shape[1:], source.dtype),
        in_specs=[pl.BlockSpec(memory_space=pltpu.SMEM), anywhere],
        out_specs=anywhere,
        scratch_shapes=[pltpu.SemaphoreType.DMA((count,))],
    )(which, source)


def per_device(features, norm_gain, row_counts, tile_cols, tile_values):
    node_dev, feat_dev = features.shape
    side = tile_values.shape[1]
    blocks = node_dev // side
    total = tile_values.shape[0]
    devices = lax.axis_size("rows")
    me = lax.axis_index("rows")
    own = features.reshape(blocks, side, feat_dev)
    peers = jnp.arange(devices, dtype=jnp.int32)
    owner = tile_cols // blocks
    local = tile_cols % blocks
    hit = owner[None, :] == peers[:, None]
    wanted = jnp.max(jnp.where(hit, local[None, :], 0), axis=1)
    requested = lax.all_to_all(
        wanted.reshape(devices, 1), "rows", split_axis=0, concat_axis=0, tiled=True
    )[:, 0]
    marked = (jnp.sum(hit.astype(jnp.int32), axis=1) >= 2) & (peers != me)
    i_am_heavy = jnp.sum(marked.astype(jnp.int32)) < HEAVY
    marked = marked | ((peers == me) & i_am_heavy)
    rank = jnp.sum((marked[None, :] & (peers[None, :] < peers[:, None])).astype(jnp.int32), axis=1)
    ranks = jnp.arange(HEAVY, dtype=jnp.int32)
    heavy_ids = jnp.sum(
        jnp.where(marked[None, :] & (rank[None, :] == ranks[:, None]), peers[None, :], 0), axis=1
    )
    outgoing = pick(jnp.where(i_am_heavy, peers % GROUP, requested), own)
    arrived = lax.all_to_all(outgoing, "rows", split_axis=0, concat_axis=0, tiled=True)
    pieces = pick(heavy_ids, arrived)
    groups = [[g * GROUP + i for i in range(GROUP)] for g in range(devices // GROUP)]
    heavy = lax.all_gather(pieces, "rows", axis_index_groups=groups, axis=0, tiled=True)
    match = owner[:, None] == heavy_ids[None, :]
    tile_rank = jnp.sum(match.astype(jnp.int32) * ranks[None, :], axis=1)
    slot = jnp.where(
        owner == me,
        devices + HEAVY * blocks + local,
        jnp.where(jnp.any(match, axis=1), devices + local * HEAVY + tile_rank, owner),
    )
    block_ids = jnp.arange(blocks, dtype=jnp.int32)
    row_ends = jnp.sum(
        jnp.where(block_ids[None, :] <= block_ids[:, None], row_counts[0][None, :], 0), axis=1
    )
    tile_index = jnp.arange(total, dtype=jnp.int32)
    row = jnp.sum((row_ends[None, :] <= tile_index[:, None]).astype(jnp.int32), axis=1)
    aggregate = tile_product(slot, row, tile_values, arrived, heavy, own)
    aggregate = aggregate.reshape(node_dev, feat_dev)
    square_sum = lax.psum(jnp.sum(aggregate * aggregate, axis=1), "feat")
    mean_square = square_sum / (feat_dev * lax.axis_size("feat"))
    return aggregate * norm_gain[None, :] * lax.rsqrt(mean_square + 1e-05)[:, None]


def solution(mesh):
    placed = (P("rows", "feat"), P("feat"), P("rows", None), P("rows"), P("rows", None, None))
    return jax.shard_map(
        per_device, mesh=mesh, in_specs=placed, out_specs=P("rows", "feat"), check_vma=False
    )
```

time: 504 us -> 601 us (1.19)
  Pallas kernels: 0 us -> 311 us
  waiting for transfers between devices: 312 us -> 236 us
  matrix products: 46.5 us -> 0 us
  local copies, waits for them, and re-layouts: 40.3 us -> 5.1 us
  other arithmetic: 40.7 us -> 6.38 us
  blocking collectives: 29.1 us -> 8.57 us
    pallas_call x0 -> x3, Pallas kernels: none -> 311 us  [the longest x2 270 us: pick(): pl.pallas_call(pick_kernel, out_shape=jax.ShapeDtypeStruct((count,) + sou...]
    psum x1 -> x0, waiting for transfers between devices: 309 us -> none  [broadcast(): return lax.psum(block, axis)]
    all_to_all x1, waiting for transfers between devices: 0.01 us -> 182 us  [per_device(): lax.all_to_all(outgoing, 'rows', split_axis=0, concat_axis=0, tiled=True)]
    dot_general x2 -> x0, matrix products: 46.5 us -> none  [the longest x1 34.4 us: per_device(): jnp.einsum('tij,tjf->tif', tile_values, picked, precision=lax.Precision.H...]
    all_gather x0 -> x1, waiting for transfers between devices: none -> 45.6 us  [per_device(): lax.all_gather(pieces, 'rows', axis_index_groups=groups, axis=0, tiled=True)]
    pmax x1 -> x0, blocking collectives: 20.5 us -> none  [per_device(): heavy_mark = lax.pmax(local_mark, 'rows')]
    gather x2 -> x0, local copies, waits for them, and re-layouts: 19.9 us -> none  [the longest x1 15.6 us: per_device(): picked = panel[panel_slot]]
    dot_general x1 -> x0, local copies, waits for them, and re-layouts: 17.6 us -> none  [per_device(): jnp.einsum('tij,tjf->tif', tile_values, picked, precision=lax.Precision.H...]
  transfers between devices with their start and end apart: 3 -> 3, of which waited for: 2 -> 3; matrix products, arithmetic and copies ran while one was open for 2% -> 0% of each run, Pallas kernels for 0% -> 0%
where the time goes in v1:
time: 601 us; the launch traced here: 600 us
  Pallas kernels  311 us (52%)
  waiting for transfers between devices  236 us (39%)
  starting transfers between devices  18.8 us (3%)
  between operations  14.2 us (2%)
  blocking collectives  8.57 us (1%)
  other arithmetic  6.38 us (1%)
    pallas_call x2, Pallas kernels, pick(): pl.pallas_call(pick_kernel, out_shape=jax.ShapeDtypeStruct((count,) + sou...  270 us
    all_to_all x1, waiting for transfers between devices, per_device(): lax.all_to_all(outgoing, 'rows', split_axis=0, concat_axis=0, tiled=True)  182 us
    all_gather x1, waiting for transfers between devices, per_device(): lax.all_gather(pieces, 'rows', axis_index_groups=groups, axis=0, tiled=True)  45.6 us
    pallas_call x1, Pallas kernels, tile_product(): pl.pallas_call(tile_kernel, out_shape=jax.ShapeDtypeStruct((blocks, side,...  41.1 us
    all_to_all x1, starting transfers between devices, per_device(): lax.all_to_all(wanted.reshape(devices, 1), 'rows', split_axis=0, concat_a...  13 us
  transfers between devices with their start and end apart: 3, of which 3 were waited for; matrix products, arithmetic and copies ran while one was open for 0% of the time, Pallas kernels for 0%

profile of v1, /device:TPU:1, one launch (start us, length us, event | category | flops | bytes accessed | tf_op | source)
XLA Modules:
  0.0 599.9 jit_solution(6936967900879405311)
XLA Ops:
  6.5 0.7 and_select_fusion.1
  7.2 0.1 select_reduce_fusion
  7.3 0.7 copy.8
  8.0 13.0 %all-to-all-start = ((s32[64,1,1]{2,1,0:T(1,128)}), s32[64,1,1]{2,1,0:T(1,128)S(1)}, u32[]{:S(2)}, u32[]{:S(2)}) async-start(s32[64,1,1]{2,1,0:T(1,128)} %copy.8), calls=%async_computation | async-start | bytes 65536 | tf_op jit(solution)/shard_map/all_to_all | solution.py:136
  21.0 0.7 convert_reduce_fusion.3
  22.4 7.9 %all-to-all-done = s32[64,1,1]{2,1,0:T(1,128)S(1)} async-done(((s32[64,1,1]{2,1,0:T(1,128)}), s32[64,1,1]{2,1,0:T(1,128)S(1)}, u32[]{:S(2)}, u32[]{:S(2)}) %all-to-all-start) | async-done | bytes 288 | tf_op jit(solution)/shard_map/all_to_all | solution.py:136
  30.3 1.2 reduce.1
  31.5 0.5 broadcast_select_fusion.which
  32.1 256.5 %shard_map.55 = f32[64,128,256]{2,1,0:T(8,128)} custom-call(s32[64]{0:T(128)} %broadcast_select_fusion.which, f32[16,128,256]{2,1,0:T(8,128)} %bitcast.8), custom_call_target="tpu_custom_call" | custom-call | tf_op jit(solution)/shard_map/pallas_call | solution.py:114
  288.5 5.8 all-to-all-start.1
  294.4 0.1 convert_reduce_fusion
  294.5 0.6 select_reduce_fusion.2.which
  295.2 182.1 %all-to-all-done.1.source.arrived = f32[64,128,256]{2,1,0:T(8,128)} async-done(((f32[64,128,256]{2,1,0:T(8,128)}), f32[64,128,256]{2,1,0:T(8,128)}, u32[]{:S(2)}, u32[]{:S(2)}) %all-to-all-start.1) | async-done | bytes 8388640 | tf_op jit(solution)/shard_map/all_to_all | solution.py:148
  477.2 13.7 %shard_map.56 = f32[3,128,256]{2,1,0:T(8,128)} custom-call(s32[3]{0:T(128)} %select_reduce_fusion.2.which, f32[64,128,256]{2,1,0:T(8,128)} %all-to-all-done.1.source.arrived), custom_call_target="tpu_custom_call" | custom-call | tf_op jit(solution)/shard_map/pallas_call | solution.py:114
  491.0 0.1 select_reduce_fusion.1
  491.1 0.1 convert_reduce_fusion.2.row
  491.3 0.1 compare_reduce_fusion
  491.4 45.6 %all-gather.2.cloned.1.call-done.heavy = f32[48,128,256]{2,1,0:T(8,128)} async-done(((f32[3,128,256]{2,1,0:T(8,128)}), f32[48,128,256]{2,1,0:T(8,128)}) %all-gather.2.cloned.1.call-update) | async-done | bytes 6291472 | tf_op jit(solution)/shard_map/all_gather | solution.py:151
  537.0 1.6 copy-done
  538.5 2.8 copy-done.1
  541.3 41.1 %shard_map.57 = f32[16,128,256]{2,1,0:T(8,128)S(1)} custom-call(s32[128]{0:T(128)S(1)} %compare_select_fusion.1.slot, s32[128]{0:T(128)S(1)} %convert_reduce_fusion.2.row, f32[128,128,128]{2,1,0:T(8,128)} %tiles.1, f32[64,128,256]{2,1,0:T(8,128)} %all-to-all-done.1.source.arrived, f32[48,128,256]{2,1,0:T(8,128)S(1)} %copy-done.1, f32[16,128,256]{2,1,0:T(8,128)S(1)} %bitcast.9), custom_call_target="tpu_custom_call" | custom-call | tf_op jit(solution)/shard_map/pallas_call | solution.py:84
  582.5 0.3 multiply_reduce_fusion
  582.8 8.6 %psum.7 = f32[2048]{0:T(1024)S(1)} all-reduce(f32[2048]{0:T(1024)S(1)} %bitcast.10), channel_id=1, replica_groups=mesh['rows'=64,'feat'=4] {'feat'}, use_global_device_ids=true, to_apply=%region_10.11 | all-reduce | flops 2048 | bytes 16384 | tf_op jit(solution)/shard_map/psum | solution.py:167
  591.4 1.7 fusion
  (14 shorter events, 0.2 us)
Async XLA Ops:
  8.0 22.3 %all-to-all-start = ((s32[64,1,1]{2,1,0:T(1,128)}), s32[64,1,1]{2,1,0:T(1,128)S(1)}, u32[]{:S(2)}, u32[]{:S(2)}) async-start(s32[64,1,1]{2,1,0:T(1,128)} %copy.8), calls=%async_computation | async-start | bytes 65536 | tf_op jit(solution)/shard_map/all_to_all | solution.py:136
  288.5 188.7 %all-to-all-start.1 = ((f32[64,128,256]{2,1,0:T(8,128)}), f32[64,128,256]{2,1,0:T(8,128)}, u32[]{:S(2)}, u32[]{:S(2)}) async-start(f32[64,128,256]{2,1,0:T(8,128)} %shard_map.55), calls=%async_computation.1 | async-start | bytes 16777216 | tf_op jit(solution)/shard_map/all_to_all | solution.py:148
  294.3 242.6 %all-gather.2.cloned.1.call-start = ((), (), s32[]{:S(2)}) async-start(), calls=%async_computation.2 | async-start | bytes 6684672 | tf_op jit(solution)/shard_map/all_gather | solution.py:151
  295.1 195.8 %copy-start.4 = (s32[1,16]{1,0:T(1,128)S(1)}, s32[1,16]{1,0:T(1,128)}, u32[]{:S(2)}) copy-start(s32[1,16]{1,0:T(1,128)} %param.7) | copy-start | bytes 196
  295.2 196.0 %copy-start.3 = (s32[3]{0:T(128)S(1)}, s32[3]{0:T(128)}, u32[]{:S(2)}) copy-start(s32[3]{0:T(128)} %select_reduce_fusion.2.which) | copy-start | bytes 40
  537.0 1.6 copy-start
  538.5 2.8 copy-start.1
  582.5 9.0 %copy-start.2 = (f32[256]{0:T(256)S(1)}, f32[256]{0:T(256)}, u32[]{:S(2)}) copy-start(f32[256]{0:T(256)} %param.6) | copy-start | bytes 3076
Sparse Core Ops, SparseCore 0:
  491.1 45.8 all-gather.1

commit v2 on v1

--- a/solution.py
+++ b/solution.py
@@ -108,14 +108,15 @@
         pltpu.make_async_copy(source.at[which[i]], out.at[i], sem.at[i]).wait()
 
 
-def pick(which, source):
+def pick(which, source, held):
     count = which.shape[0]
-    anywhere = pl.BlockSpec(memory_space=pl.ANY)
+    spaces = (pltpu.VMEM, pl.ANY) if held else (pl.ANY, pltpu.VMEM)
+    inner, outer = [pl.BlockSpec(memory_space=space) for space in spaces]
     return pl.pallas_call(
         pick_kernel,
         out_shape=jax.ShapeDtypeStruct((count,) + source.shape[1:], source.dtype),
-        in_specs=[pl.BlockSpec(memory_space=pltpu.SMEM), anywhere],
-        out_specs=anywhere,
+        in_specs=[pl.BlockSpec(memory_space=pltpu.SMEM), inner],
+        out_specs=outer,
         scratch_shapes=[pltpu.SemaphoreType.DMA((count,))],
     )(which, source)
 
@@ -144,9 +145,9 @@
     heavy_ids = jnp.sum(
         jnp.where(marked[None, :] & (rank[None, :] == ranks[:, None]), peers[None, :], 0), axis=1
     )
-    outgoing = pick(jnp.where(i_am_heavy, peers % GROUP, requested), own)
+    outgoing = pick(jnp.where(i_am_heavy, peers % GROUP, requested), own, True)
     arrived = lax.all_to_all(outgoing, "rows", split_axis=0, concat_axis=0, tiled=True)
-    pieces = pick(heavy_ids, arrived)
+    pieces = pick(heavy_ids, arrived, False)
     groups = [[g * GROUP + i for i in range(GROUP)] for g in range(devices // GROUP)]
     heavy = lax.all_gather(pieces, "rows", axis_index_groups=groups, axis=0, tiled=True)
     match = owner[:, None] == heavy_ids[None, :]

time: 601 us -> 339 us (0.56)
  Pallas kernels: 311 us -> 49 us
    pallas_call x2, Pallas kernels: 270 us -> 7.86 us  [pick(): pl.pallas_call(pick_kernel, out_shape=jax.ShapeDtypeStruct((count,) + sou...]
  transfers between devices with their start and end apart: 3 -> 3, of which waited for: 3 -> 3; matrix products, arithmetic and copies ran while one was open for 0% -> 1% of each run, Pallas kernels for 0% -> 0%
where the time goes in v2:
time: 339 us; the launch traced here: 338 us
  waiting for transfers between devices  236 us (70%)
  Pallas kernels  49 us (14%)
  starting transfers between devices  18.8 us (6%)
  between operations  14.2 us (4%)
  blocking collectives  8.57 us (3%)
  other arithmetic  6.38 us (2%)
  local copies, waits for them, and re-layouts  5.1 us (2%)
    all_to_all x1, waiting for transfers between devices, per_device(): lax.all_to_all(outgoing, 'rows', split_axis=0, concat_axis=0, tiled=True)  182 us
    all_gather x1, waiting for transfers between devices, per_device(): lax.all_gather(pieces, 'rows', axis_index_groups=groups, axis=0, tiled=True)  45.6 us
    pallas_call x1, Pallas kernels, tile_product(): pl.pallas_call(tile_kernel, out_shape=jax.ShapeDtypeStruct((blocks, side,...  41.1 us
    all_to_all x1, starting transfers between devices, per_device(): lax.all_to_all(wanted.reshape(devices, 1), 'rows', split_axis=0, concat_a...  13 us
    psum x1, blocking collectives, per_device(): square_sum = lax.psum(jnp.sum(aggregate * aggregate, axis=1), 'feat')  8.57 us
    all_to_all x1, waiting for transfers between devices, per_device(): lax.all_to_all(wanted.reshape(devices, 1), 'rows', split_axis=0, concat_a...  7.89 us
    pallas_call x2, Pallas kernels, pick(): pl.pallas_call(pick_kernel, out_shape=jax.ShapeDtypeStruct((count,) + sou...  7.86 us
  transfers between devices with their start and end apart: 3, of which 3 were waited for; matrix products, arithmetic and copies ran while one was open for 1% of the time, Pallas kernels for 0%

profile of v2, /device:TPU:1, one launch (start us, length us, event | category | flops | bytes accessed | tf_op | source)
XLA Modules:
  0.0 337.6 jit_solution(767517784492537330)
XLA Ops:
  6.5 0.7 and_select_fusion.1
  7.2 0.1 select_reduce_fusion
  7.3 0.7 copy.8
  8.0 13.0 %all-to-all-start = ((s32[64,1,1]{2,1,0:T(1,128)}), s32[64,1,1]{2,1,0:T(1,128)S(1)}, u32[]{:S(2)}, u32[]{:S(2)}) async-start(s32[64,1,1]{2,1,0:T(1,128)} %copy.8), calls=%async_computation | async-start | bytes 65536 | tf_op jit(solution)/shard_map/all_to_all | solution.py:137
  21.0 0.7 convert_reduce_fusion.3
  22.4 7.9 %all-to-all-done = s32[64,1,1]{2,1,0:T(1,128)S(1)} async-done(((s32[64,1,1]{2,1,0:T(1,128)}), s32[64,1,1]{2,1,0:T(1,128)S(1)}, u32[]{:S(2)}, u32[]{:S(2)}) %all-to-all-start) | async-done | bytes 288 | tf_op jit(solution)/shard_map/all_to_all | solution.py:137
  30.3 1.2 reduce.1
  31.5 0.5 broadcast_select_fusion.which
  32.1 5.4 %shard_map.55 = f32[64,128,256]{2,1,0:T(8,128)} custom-call(s32[64]{0:T(128)} %broadcast_select_fusion.which, f32[16,128,256]{2,1,0:T(8,128)} %bitcast.8), custom_call_target="tpu_custom_call" | custom-call | tf_op jit(solution)/shard_map/pallas_call | solution.py:115
  37.5 5.8 %all-to-all-start.1 = ((f32[64,128,256]{2,1,0:T(8,128)}), f32[64,128,256]{2,1,0:T(8,128)}, u32[]{:S(2)}, u32[]{:S(2)}) async-start(f32[64,128,256]{2,1,0:T(8,128)} %shard_map.55), calls=%async_computation.1 | async-start | bytes 16777216 | tf_op jit(solution)/shard_map/all_to_all | solution.py:149
  43.3 0.1 convert_reduce_fusion
  43.4 0.6 select_reduce_fusion.2.which
  44.1 182.1 %all-to-all-done.1.source.arrived = f32[64,128,256]{2,1,0:T(8,128)} async-done(((f32[64,128,256]{2,1,0:T(8,128)}), f32[64,128,256]{2,1,0:T(8,128)}, u32[]{:S(2)}, u32[]{:S(2)}) %all-to-all-start.1) | async-done | bytes 8388640 | tf_op jit(solution)/shard_map/all_to_all | solution.py:149
  226.2 2.5 shard_map.56
  228.7 0.1 select_reduce_fusion.1
  228.8 0.1 convert_reduce_fusion.2.row
  229.0 0.1 compare_reduce_fusion
  229.1 45.6 %all-gather.2.cloned.1.call-done.heavy = f32[48,128,256]{2,1,0:T(8,128)} async-done(((f32[3,128,256]{2,1,0:T(8,128)}), f32[48,128,256]{2,1,0:T(8,128)}) %all-gather.2.cloned.1.call-update) | async-done | bytes 6291472 | tf_op jit(solution)/shard_map/all_gather | solution.py:152
  274.7 1.6 copy-done
  276.2 2.8 copy-done.1
  279.0 41.1 %shard_map.57 = f32[16,128,256]{2,1,0:T(8,128)S(1)} custom-call(s32[128]{0:T(128)S(1)} %compare_select_fusion.1.slot, s32[128]{0:T(128)S(1)} %convert_reduce_fusion.2.row, f32[128,128,128]{2,1,0:T(8,128)} %tiles.1, f32[64,128,256]{2,1,0:T(8,128)} %all-to-all-done.1.source.arrived, f32[48,128,256]{2,1,0:T(8,128)S(1)} %copy-done.1, f32[16,128,256]{2,1,0:T(8,128)S(1)} %bitcast.9), custom_call_target="tpu_custom_call" | custom-call | tf_op jit(solution)/shard_map/pallas_call | solution.py:84
  320.2 0.3 multiply_reduce_fusion
  320.5 8.6 %psum.7 = f32[2048]{0:T(1024)S(1)} all-reduce(f32[2048]{0:T(1024)S(1)} %bitcast.10), channel_id=1, replica_groups=mesh['rows'=64,'feat'=4] {'feat'}, use_global_device_ids=true, to_apply=%region_10.11 | all-reduce | flops 2048 | bytes 16384 | tf_op jit(solution)/shard_map/psum | solution.py:168
  329.1 1.7 fusion
  (14 shorter events, 0.2 us)
Async XLA Ops:
  8.0 22.3 %all-to-all-start = ((s32[64,1,1]{2,1,0:T(1,128)}), s32[64,1,1]{2,1,0:T(1,128)S(1)}, u32[]{:S(2)}, u32[]{:S(2)}) async-start(s32[64,1,1]{2,1,0:T(1,128)} %copy.8), calls=%async_computation | async-start | bytes 65536 | tf_op jit(solution)/shard_map/all_to_all | solution.py:137
  37.5 188.7 %all-to-all-start.1 = ((f32[64,128,256]{2,1,0:T(8,128)}), f32[64,128,256]{2,1,0:T(8,128)}, u32[]{:S(2)}, u32[]{:S(2)}) async-start(f32[64,128,256]{2,1,0:T(8,128)} %shard_map.55), calls=%async_computation.1 | async-start | bytes 16777216 | tf_op jit(solution)/shard_map/all_to_all | solution.py:149
  43.3 231.4 %all-gather.2.cloned.1.call-start = ((), (), s32[]{:S(2)}) async-start(), calls=%async_computation.2 | async-start | bytes 6684672 | tf_op jit(solution)/shard_map/all_gather | solution.py:152
  44.1 184.6 %copy-start.4 = (s32[1,16]{1,0:T(1,128)S(1)}, s32[1,16]{1,0:T(1,128)}, u32[]{:S(2)}) copy-start(s32[1,16]{1,0:T(1,128)} %param.7) | copy-start | bytes 196
  44.1 184.8 %copy-start.3 = (s32[3]{0:T(128)S(1)}, s32[3]{0:T(128)}, u32[]{:S(2)}) copy-start(s32[3]{0:T(128)} %select_reduce_fusion.2.which) | copy-start | bytes 40
  274.7 1.6 copy-start
  276.2 2.8 copy-start.1
  320.2 9.0 %copy-start.2 = (f32[256]{0:T(256)S(1)}, f32[256]{0:T(256)}, u32[]{:S(2)}) copy-start(f32[256]{0:T(256)} %param.6) | copy-start | bytes 3076
Sparse Core Ops, SparseCore 0:
  228.8 45.8 all-gather.1

commit v3 on v1

--- a/solution.py
+++ b/solution.py
@@ -15,7 +15,8 @@
 
 def tile_kernel(slot, row, tiles, arrived, heavy, own, out, abuf, xbuf, asem, xsem):
     total = tiles.shape[0]
-    n_arr, n_heavy = arrived.shape[0], heavy.shape[0]
+    n_arr, n_heavy = arrived.shape[1], heavy.shape[1]
+    side, feat = own.shape[1] * own.shape[2], own.shape[3]
 
     def tile_copy(c):
         part = pl.ds(c * CHUNK, CHUNK)
@@ -26,11 +27,11 @@
 
         @pl.when(s < n_arr)
         def _():
-            pltpu.make_async_copy(arrived.at[s], xbuf.at[b], xsem.at[b]).start()
+            pltpu.make_async_copy(arrived.at[:, s], xbuf.at[b], xsem.at[b]).start()
 
         @pl.when((s >= n_arr) & (s < n_arr + n_heavy))
         def _():
-            pltpu.make_async_copy(heavy.at[s - n_arr], xbuf.at[b], xsem.at[b]).start()
+            pltpu.make_async_copy(heavy.at[:, s - n_arr], xbuf.at[b], xsem.at[b]).start()
 
         @pl.when(s >= n_arr + n_heavy)
         def _():
@@ -57,9 +58,9 @@
         def _():
             tile_copy(t // CHUNK).wait()
 
-        pltpu.make_async_copy(arrived.at[0], xbuf.at[b], xsem.at[b]).wait()
+        pltpu.make_async_copy(arrived.at[:, 0], xbuf.at[b], xsem.at[b]).wait()
         a = abuf[t]
-        x = jnp.maximum(xbuf[b], 0.0)
+        x = jnp.maximum(xbuf[b].reshape(side, feat), 0.0)
         a_hi = a.astype(jnp.bfloat16)
         a_lo = (a - a_hi.astype(jnp.float32)).astype(jnp.bfloat16)
         x_hi = x.astype(jnp.bfloat16)
@@ -88,36 +89,255 @@
         out_specs=pl.BlockSpec(memory_space=pltpu.VMEM),
         scratch_shapes=[
             pltpu.VMEM(tiles.shape, jnp.float32),
-            pltpu.VMEM((DEPTH, side, feat), jnp.float32),
+            pltpu.VMEM((DEPTH, PARTS, side // PARTS, feat), jnp.float32),
             pltpu.SemaphoreType.DMA((total // CHUNK,)),
             pltpu.SemaphoreType.DMA((DEPTH,)),
         ],
         compiler_params=pltpu.CompilerParams(vmem_limit_bytes=40 << 20),
-    )(slot, row, tiles, arrived, heavy, own)
-
-
-def pick_kernel(which, source, out, sem):
-    count = out.shape[0]
-
-    @pl.loop(0, count)
-    def _(i):
-        pltpu.make_async_copy(source.at[which[i]], out.at[i], sem.at[i]).start()
-
-    @pl.loop(0, count)
-    def _(i):
-        pltpu.make_async_copy(source.at[which[i]], out.at[i], sem.at[i]).wait()
-
-
-def pick(which, source):
-    count = which.shape[0]
+    )(slot, row, tiles, arrived, heavy, own.reshape(blocks, PARTS, side // PARTS, feat))
+
+
+PARTS = 4
+PLANE = 8
+PLANES = 8
+MESH = pl.DeviceIdType.MESH
+
+
+def exchange_kernel(table, heavy_slot, features, arrived_out, heavy_out, *scratch):
+    names = ("own", "up1", "down1", "up2", "down2", "up3s", "down3s", "up3", "down3", "far", "picked", "arrived", "gathered")
+    bufs = {n: scratch[i * PARTS : (i + 1) * PARTS] for i, n in enumerate(names)}
+    own, up1, down1, up2, down2, up3s, down3s, up3, down3, far, picked, arrived, gathered = (bufs[n] for n in names)
+    load_sem, zs, zr, xs, xr, gs, gr, out_sem = scratch[len(names) * PARTS :]
+    me = lax.axis_index("rows")
+    z, q = me // PLANE, lax.rem(me, PLANE)
+    x, c = q // 2, lax.rem(q, 2)
+    part_rows = own[0].shape[1]
+
+    def at(dz):
+        return lax.rem(z + dz + PLANES, PLANES)
+
+    up, down = at(1) * PLANE + q, at(-1) * PLANE + q
+    even = 1 - lax.rem(z, 2)
+    partner = (z + 2 * even - 1) * PLANE + q
+    right = z * PLANE + lax.rem(x + 1, 4) * 2 + c
+    left = z * PLANE + lax.rem(x + 3, 4) * 2 + c
+    other = z * PLANE + x * 2 + 1 - c
+
+    def load(k):
+        return pltpu.make_async_copy(features.at[:, pl.ds(k * part_rows, part_rows)], own[k], load_sem.at[k])
+
+    for k in range(PARTS):
+        load(k).start()
+    barrier = pltpu.get_barrier_semaphore()
+    for peer in (up, down):
+        pl.semaphore_signal(barrier, inc=1, device_id={"rows": peer}, device_id_type=MESH)
+
+    @pl.loop(1, PLANE)
+    def _(p):
+        peer = z * PLANE + lax.rem(q + p, PLANE)
+        pl.semaphore_signal(barrier, inc=1, device_id={"rows": peer}, device_id_type=MESH)
+
+    pl.semaphore_wait(barrier, PLANE + 1)
+
+    def send(src, dst, ssem, rsem, peer):
+        return pltpu.make_async_remote_copy(
+            src_ref=src, dst_ref=dst, send_sem=ssem, recv_sem=rsem, device_id={"rows": peer}, device_id_type=MESH
+        )
+
+    def z_copies(k, step):
+        src_up, dst_up, src_down, dst_down = (
+            (own[k], up1[k], own[k], down1[k]),
+            (up1[k], up2[k], down1[k], down2[k]),
+            (up3s[k], up3[k], down3s[k], down3[k]),
+            (up3[k].at[pl.ds(PLANE, 4)], far[k].at[0], down3[k].at[pl.ds(PLANE, 4)], far[k].at[1]),
+        )[step]
+        i = (k * 4 + step) * 2
+        return (
+            send(src_up, dst_up, zs.at[i], zr.at[i], up),
+            send(src_down, dst_down, zs.at[i + 1], zr.at[i + 1], down),
+        )
+
+    def z_start(k, step):
+        for copy in z_copies(k, step):
+            copy.start()
+
+    def z_wait(k, step):
+        for copy in z_copies(k, step):
+            copy.wait_recv()
+
+    def block_of(dz_reader, reader, dz_owner):
+        return table[(at(dz_reader) * PLANE + reader) * (PLANES * PLANE) + at(dz_owner) * PLANE + q]
+
+    def x_pick(k, first, sources):
+        @pl.loop(0, PLANE)
+        def _(reader):
+            for i, (ref, dz) in enumerate(sources):
+                picked[k][reader, first + i] = ref[block_of(0, reader, dz)]
+
+        arrived[k][pl.ds(q * PLANES + first, len(sources))] = picked[k][q, pl.ds(first, len(sources))]
+
+        @pl.loop(1, PLANE)
+        def _(p):
+            reader = lax.rem(q + p, PLANE)
+            send(
+                picked[k].at[reader, pl.ds(first, len(sources))],
+                arrived[k].at[pl.ds(q * PLANES + first, len(sources))],
+                xs.at[k],
+                xr.at[k],
+                z * PLANE + reader,
+            ).start()
+
+    def x_pass(k, first, source):
+        arrived[k][q * PLANES + first] = source(q)[...]
+
+        @pl.loop(1, PLANE)
+        def _(p):
+            reader = lax.rem(q + p, PLANE)
+            send(source(reader), arrived[k].at[q * PLANES + first], xs.at[k], xr.at[k], z * PLANE + reader).start()
+
+    def gather_copy(k, i, src, dst, peer):
+        j = k * 8 + i
+        return send(src, dst, gs.at[j], gr.at[j], peer)
+
+    def mine(k, qq):
+        return gathered[k].at[qq]
+
+    def q_of(xx):
+        return lax.rem(x + xx + 4, 4) * 2 + c
+
+    def gather_copies(k, i):
+        if i == 0:
+            src = gathered[k].at[q, 1 - even]
+            return gather_copy(k, 0, src, src, partner)
+        if i == 1:
+            return gather_copy(k, 1, mine(k, q), mine(k, q), right)
+        if i == 2:
+            return gather_copy(k, 2, mine(k, q), mine(k, q), left)
+        if i == 3:
+            src = gathered[k].at[q_of(-1), 0]
+            return gather_copy(k, 3, src, src, right)
+        if i == 4:
+            src = gathered[k].at[q_of(1), 1]
+            return gather_copy(k, 4, src, src, left)
+        src = mine(k, q_of((0, 1, -1)[i - 5])) if i < 8 else None
+        return gather_copy(k, i, src, src, other)
+
+    def last_core_copy(k):
+        src = mine(k, q_of(2))
+        j = PARTS * 8 + k
+        return send(src, src, gs.at[j], gr.at[j], other)
+
+    def arrived_store(k):
+        return pltpu.make_async_copy(arrived[k], arrived_out.at[k], out_sem.at[k])
+
+    def heavy_store(k):
+        return pltpu.make_async_copy(gathered[k], heavy_out.at[k], out_sem.at[PARTS + k])
+
+    def stage(k, s):
+        if s == 0:
+            load(k).wait()
+            z_start(k, 0)
+            x_pick(k, 0, [(own[k], 0)])
+        elif s == 1:
+            z_wait(k, 0)
+            z_start(k, 1)
+            x_pick(k, 1, [(up1[k], -1), (down1[k], 1)])
+        elif s == 2:
+            z_wait(k, 1)
+
+            @pl.loop(0, PLANE)
+            def _(reader):
+                up3s[k][reader] = up2[k][block_of(1, reader, -2)]
+                down3s[k][reader] = down2[k][block_of(-1, reader, 2)]
+
+            @pl.loop(0, 4)
+            def _(half):
+                up3s[k][PLANE + half] = up2[k][block_of(2, 2 * half, -2)]
+                down3s[k][PLANE + half] = down2[k][block_of(-2, 2 * half + 1, 2)]
+
+            z_start(k, 2)
+            x_pick(k, 3, [(up2[k], -2), (down2[k], 2)])
+        elif s == 3:
+            z_wait(k, 2)
+            z_start(k, 3)
+            x_pass(k, 5, lambda reader: up3[k].at[reader])
+            x_pass(k, 6, lambda reader: down3[k].at[reader])
+        elif s == 4:
+            z_wait(k, 3)
+            x_pass(k, 7, lambda reader: far[k].at[lax.rem(reader, 2), reader // 2])
+        elif s == 5:
+            everything = arrived[k].at[pl.ds(0, (PLANE - 1) * PLANES)]
+            pltpu.make_async_copy(everything, everything, xr.at[k]).wait()
+            arrived_store(k).start()
+            for i in range(HEAVY):
+                gathered[k][q, 1 - even, i] = arrived[k][heavy_slot[i]]
+            gather_copies(k, 0).start()
+        elif s == 6:
+            gather_copies(k, 0).wait_recv()
+            for i in (1, 2, 5):
+                gather_copies(k, i).start()
+        elif s == 7:
+            gather_copies(k, 1).wait_recv()
+            gather_copies(k, 2).wait_recv()
+            for i in (3, 4, 6, 7):
+                gather_copies(k, i).start()
+        elif s == 8:
+            gather_copies(k, 3).wait_recv()
+            gather_copies(k, 4).wait_recv()
+            last_core_copy(k).start()
+        elif s == 9:
+            for i in (5, 6, 7):
+                gather_copies(k, i).wait_recv()
+            last_core_copy(k).wait_recv()
+            heavy_store(k).start()
+
+    for t in range(PARTS + 9):
+        for s in range(10):
+            if 0 <= t - s < PARTS:
+                stage(t - s, s)
+
+    for k in range(PARTS):
+        for step in range(4):
+            for copy in z_copies(k, step):
+                copy.wait_send()
+        everything = arrived[k].at[pl.ds(0, (PLANE - 1) * PLANES)]
+        pltpu.make_async_copy(everything, everything, xs.at[k]).wait()
+        for i in range(8):
+            gather_copies(k, i).wait_send()
+        last_core_copy(k).wait_send()
+        arrived_store(k).wait()
+        heavy_store(k).wait()
+
+
+def exchange(table, heavy_slot, own):
+    blocks, side, feat = own.shape
+    rows = side // PARTS
+    smem = pl.BlockSpec(memory_space=pltpu.SMEM)
     anywhere = pl.BlockSpec(memory_space=pl.ANY)
+    leads = [(blocks,)] * 5 + [(PLANE + 4,)] * 4 + [(2, 4), (PLANE, 5), (PLANE * PLANES,), (PLANE, 2, HEAVY)]
+    bufs = [pltpu.VMEM(lead + (rows, feat), jnp.float32) for lead in leads for _ in range(PARTS)]
+    dma = pltpu.SemaphoreType.DMA
     return pl.pallas_call(
-        pick_kernel,
-        out_shape=jax.ShapeDtypeStruct((count,) + source.shape[1:], source.dtype),
-        in_specs=[pl.BlockSpec(memory_space=pltpu.SMEM), anywhere],
-        out_specs=anywhere,
-        scratch_shapes=[pltpu.SemaphoreType.DMA((count,))],
-    )(which, source)
+        exchange_kernel,
+        out_shape=[
+            jax.ShapeDtypeStruct((PARTS, PLANE * PLANES, rows, feat), jnp.float32),
+            jax.ShapeDtypeStruct((PARTS, PLANE, 2, HEAVY, rows, feat), jnp.float32),
+        ],
+        in_specs=[smem, smem, anywhere],
+        out_specs=[anywhere, anywhere],
+        scratch_shapes=bufs
+        + [
+            dma((PARTS,)),
+            dma((PARTS * 8,)),
+            dma((PARTS * 8,)),
+            dma((PARTS,)),
+            dma((PARTS,)),
+            dma((PARTS * 9,)),
+            dma((PARTS * 9,)),
+            dma((PARTS * 2,)),
+        ],
+        compiler_params=pltpu.CompilerParams(collective_id=0, has_side_effects=True, vmem_limit_bytes=56 << 20),
+    )(table, heavy_slot, own)
 
 
 def per_device(features, norm_gain, row_counts, tile_cols, tile_values):
@@ -133,9 +353,6 @@
     local = tile_cols % blocks
     hit = owner[None, :] == peers[:, None]
     wanted = jnp.max(jnp.where(hit, local[None, :], 0), axis=1)
-    requested = lax.all_to_all(
-        wanted.reshape(devices, 1), "rows", split_axis=0, concat_axis=0, tiled=True
-    )[:, 0]
     marked = (jnp.sum(hit.astype(jnp.int32), axis=1) >= 2) & (peers != me)
     i_am_heavy = jnp.sum(marked.astype(jnp.int32)) < HEAVY
     marked = marked | ((peers == me) & i_am_heavy)
@@ -144,17 +361,25 @@
     heavy_ids = jnp.sum(
         jnp.where(marked[None, :] & (rank[None, :] == ranks[:, None]), peers[None, :], 0), axis=1
     )
-    outgoing = pick(jnp.where(i_am_heavy, peers % GROUP, requested), own)
-    arrived = lax.all_to_all(outgoing, "rows", split_axis=0, concat_axis=0, tiled=True)
-    pieces = pick(heavy_ids, arrived)
-    groups = [[g * GROUP + i for i in range(GROUP)] for g in range(devices // GROUP)]
-    heavy = lax.all_gather(pieces, "rows", axis_index_groups=groups, axis=0, tiled=True)
+    wanted = jnp.where(marked | (peers == me), me % GROUP, wanted)
+    table = lax.all_gather(wanted, "rows", axis=0, tiled=True)
+
+    def panel_slot(stripe):
+        ahead = (stripe // PLANE - me // PLANE + PLANES) % PLANES
+        return stripe % PLANE * PLANES + jnp.where(ahead < 4, 2 * ahead, 2 * (PLANES - ahead) - 1)
+
+    arrived, heavy = exchange(table, panel_slot(heavy_ids), own)
+    heavy = heavy.reshape((PARTS, blocks * HEAVY) + heavy.shape[-2:])
     match = owner[:, None] == heavy_ids[None, :]
     tile_rank = jnp.sum(match.astype(jnp.int32) * ranks[None, :], axis=1)
     slot = jnp.where(
         owner == me,
         devices + HEAVY * blocks + local,
-        jnp.where(jnp.any(match, axis=1), devices + local * HEAVY + tile_rank, owner),
+        jnp.where(
+            jnp.any(match, axis=1),
+            devices + (local % PLANE * 2 + local // PLANE) * HEAVY + tile_rank,
+            panel_slot(owner),
+        ),
     )
     block_ids = jnp.arange(blocks, dtype=jnp.int32)
     row_ends = jnp.sum(

time: 601 us -> 484 us (0.81)
  blocking collectives: 8.57 us -> 258 us
  waiting for transfers between devices: 236 us -> 0 us
  Pallas kernels: 311 us -> 213 us
  starting transfers between devices: 18.8 us -> 0 us
  between operations: 14.2 us -> 1.44 us
    unnamed x0 -> x1, blocking collectives: none -> 249 us
    all_to_all x2 -> x0, waiting for transfers between devices: 190 us -> none  [the longest x1 182 us: per_device(): lax.all_to_all(outgoing, 'rows', split_axis=0, concat_axis=0, tiled=True)]
    pallas_call x2 -> x1, Pallas kernels: 270 us -> 179 us  [exchange(): pl.pallas_call(exchange_kernel, out_shape=[jax.ShapeDtypeStruct((PARTS, P...]
    all_gather x1 -> x0, waiting for transfers between devices: 45.6 us -> none  [per_device(): lax.all_gather(pieces, 'rows', axis_index_groups=groups, axis=0, tiled=True)]
    all_to_all x2 -> x0, starting transfers between devices: 18.8 us -> none  [the longest x1 13 us: per_device(): lax.all_to_all(wanted.reshape(devices, 1), 'rows', split_axis=0, concat_a...]
    pallas_call x1, Pallas kernels: 41.1 us -> 33.5 us  [tile_product(): pl.pallas_call(tile_kernel, out_shape=jax.ShapeDtypeStruct((blocks, side,...]
  transfers between devices with their start and end apart: 3 -> 0, of which waited for: 3 -> 0; matrix products, arithmetic and copies ran while one was open for 0% -> 0% of each run, Pallas kernels for 0% -> 0%
where the time goes in v3:
time: 484 us; the launch traced here: 482 us
  blocking collectives  258 us (53%)
  Pallas kernels  213 us (44%)
  other arithmetic  5.53 us (1%)
    unnamed x1, blocking collectives  249 us
    pallas_call x1, Pallas kernels, exchange(): pl.pallas_call(exchange_kernel, out_shape=[jax.ShapeDtypeStruct((PARTS, P...  179 us
    pallas_call x1, Pallas kernels, tile_product(): pl.pallas_call(tile_kernel, out_shape=jax.ShapeDtypeStruct((blocks, side,...  33.5 us

profile of v3, /device:TPU:1, one launch (start us, length us, event | category | flops | bytes accessed | tf_op | source)
XLA Modules:
  0.0 482.0 jit_solution(800115621361166677)
XLA Ops:
  0.0 1.3 dynamic-slice
  1.9 0.8 select_reduce_fusion.1
  2.7 0.1 convert_reduce_fusion.2.row
  2.8 0.7 and_select_fusion.8
  3.4 0.1 select_reduce_fusion
  3.6 0.7 convert_reduce_fusion.3
  5.0 0.1 fusion.9
  5.1 249.4 %all-reduce.table = s32[4096]{0:T(1024)} all-reduce(s32[4096]{0:T(1024)S(1)} %get-tuple-element.11), channel_id=1, replica_groups=mesh['rows'=64,'feat'=4] {'rows'}, use_global_device_ids=true, to_apply=%add | all-reduce | flops 4096 | bytes 32768
  254.5 0.0 copy-start
  254.5 0.1 convert_reduce_fusion
  254.7 0.1 select_reduce_fusion.2
  254.8 0.1 fusion.2
  254.9 0.6 fusion.11.heavy_slot
  255.5 0.1 compare_reduce_fusion
  255.6 179.2 %shard_map.55 = (f32[4,64,32,256]{3,2,1,0:T(8,128)}, f32[4,8,2,3,32,256]{5,4,3,2,1,0:T(8,128)}) custom-call(s32[4096]{0:T(1024)} %all-reduce.table, s32[3]{0:T(128)} %fusion.11.heavy_slot, f32[16,128,256]{2,1,0:T(8,128)} %bitcast.10), custom_call_target="tpu_custom_call" | custom-call | tf_op jit(solution)/shard_map/pallas_call | solution.py:320
  434.8 0.0 copy-done
  434.8 0.0 copy-start.1
  434.8 2.8 copy-done.1
  437.6 33.5 %shard_map.56 = f32[16,128,256]{2,1,0:T(8,128)S(1)} custom-call(s32[128]{0:T(128)S(1)} %compare_select_fusion.7.slot, s32[128]{0:T(128)S(1)} %convert_reduce_fusion.2.row, f32[128,128,128]{2,1,0:T(8,128)} %tiles.1, f32[4,64,32,256]{3,2,1,0:T(8,128)} %get-tuple-element.7.arrived, f32[4,48,32,256]{3,2,1,0:T(8,128)S(1)} %bitcast.12, f32[16,4,32,256]{3,2,1,0:T(8,128)S(1)} %bitcast.11), custom_call_target="tpu_custom_call" | custom-call | tf_op jit(solution)/shard_map/pallas_call | solution.py:85
  471.1 0.0 copy-start.2
  471.1 0.3 multiply_reduce_fusion
  471.4 8.8 %psum.7 = f32[2048]{0:T(1024)S(1)} all-reduce(f32[2048]{0:T(1024)S(1)} %bitcast.13), channel_id=1, replica_groups=mesh['rows'=64,'feat'=4] {'feat'}, use_global_device_ids=true, to_apply=%region_10.11 | all-reduce | flops 2048 | bytes 16384 | tf_op jit(solution)/shard_map/psum | solution.py:392
  480.3 0.0 copy-done.2
  480.3 1.7 fusion
  (3 shorter events, 0.0 us)
Async XLA Ops:
  254.5 180.3 %copy-start = (f32[2048,256]{1,0:T(8,128)S(1)}, f32[2048,256]{1,0:T(8,128)}, u32[]{:S(2)}) copy-start(f32[2048,256]{1,0:T(8,128)} %param.5) | copy-start | bytes 6291460
  434.8 2.8 copy-start.1
  471.1 9.2 %copy-start.2 = (f32[256]{0:T(256)S(1)}, f32[256]{0:T(256)}, u32[]{:S(2)}) copy-start(f32[256]{0:T(256)} %param.6) | copy-start | bytes 3076

commit v4 on v3

--- a/solution.py
+++ b/solution.py
@@ -13,7 +13,7 @@
 CHUNK = 8
 
 
-def tile_kernel(slot, row, tiles, arrived, heavy, own, out, abuf, xbuf, asem, xsem):
+def tile_kernel(plan, tiles, arrived, heavy, own, out, abuf, xbuf, asem, xsem):
     total = tiles.shape[0]
     n_arr, n_heavy = arrived.shape[1], heavy.shape[1]
     side, feat = own.shape[1] * own.shape[2], own.shape[3]
@@ -23,7 +23,7 @@
         return pltpu.make_async_copy(tiles.at[part], abuf.at[part], asem.at[c])
 
     def fetch(t):
-        s, b = slot[t], lax.rem(t, DEPTH)
+        s, b = plan[0, t], lax.rem(t, DEPTH)
 
         @pl.when(s < n_arr)
         def _():
@@ -70,14 +70,14 @@
             jnp.concatenate([x_hi, x_hi], axis=0),
             preferred_element_type=jnp.float32,
         ) + jnp.dot(a_hi, x_lo, preferred_element_type=jnp.float32)
-        out[row[t]] += prod
+        out[plan[1, t]] += prod
 
         @pl.when(t + DEPTH < total)
         def _():
             fetch(t + DEPTH)
 
 
-def tile_product(slot, row, tiles, arrived, heavy, own):
+def tile_product(plan, tiles, arrived, heavy, own):
     blocks, side, feat = own.shape
     total = tiles.shape[0]
     smem = pl.BlockSpec(memory_space=pltpu.SMEM)
@@ -85,7 +85,7 @@
     return pl.pallas_call(
         tile_kernel,
         out_shape=jax.ShapeDtypeStruct((blocks, side, feat), jnp.float32),
-        in_specs=[smem, smem, anywhere, anywhere, anywhere, anywhere],
+        in_specs=[smem, anywhere, anywhere, anywhere, anywhere],
         out_specs=pl.BlockSpec(memory_space=pltpu.VMEM),
         scratch_shapes=[
             pltpu.VMEM(tiles.shape, jnp.float32),
@@ -94,7 +94,7 @@
             pltpu.SemaphoreType.DMA((DEPTH,)),
         ],
         compiler_params=pltpu.CompilerParams(vmem_limit_bytes=40 << 20),
-    )(slot, row, tiles, arrived, heavy, own.reshape(blocks, PARTS, side // PARTS, feat))
+    )(plan, tiles, arrived, heavy, own.reshape(blocks, PARTS, side // PARTS, feat))
 
 
 PARTS = 4
@@ -103,11 +103,55 @@
 MESH = pl.DeviceIdType.MESH
 
 
-def exchange_kernel(table, heavy_slot, features, arrived_out, heavy_out, *scratch):
+def total_of(mask, values, axis):
+    return jnp.sum(jnp.where(mask, values, 0), axis=axis, keepdims=True)
+
+
+def plan_rows(me, cols, counts, blocks):
+    lanes = cols.shape[1]
+    devices, shift = PLANE * PLANES, blocks.bit_length() - 1
+    i = lax.broadcasted_iota(jnp.int32, (lanes, lanes), 0)
+    j = lax.broadcasted_iota(jnp.int32, (lanes, lanes), 1)
+    lane, down = j[:1], i[:, :1]
+
+    def panel_slot(stripe):
+        ahead = ((stripe >> 3) - me // PLANE + PLANES) & (PLANES - 1)
+        return (stripe & (PLANE - 1)) * PLANES + jnp.where(ahead < 4, 2 * ahead, 2 * (PLANES - ahead) - 1)
+
+    spread = jnp.broadcast_to(cols, (lanes, lanes))
+    turned = spread.T
+    hit = (turned >> shift) == j
+    wanted = jnp.max(jnp.where(hit, turned & (blocks - 1), 0), axis=0, keepdims=True)
+    marked = (total_of(hit, 1, 0) >= 2) & (lane != me)
+    i_am_heavy = total_of(marked, 1, 1) < HEAVY
+    marked = marked | ((lane == me) & i_am_heavy)
+    hit_down = (spread >> shift) == i
+    marked_down = (total_of(hit_down, 1, 1) >= 2) & (down != me)
+    marked_down = marked_down | ((down == me) & i_am_heavy)
+    rank = total_of(jnp.broadcast_to(marked_down, i.shape) & (i < j), 1, 0)
+    rank_down = total_of(jnp.broadcast_to(marked, i.shape) & (j < i), 1, 1)
+    request = jnp.where(marked | (lane == me), me & (GROUP - 1), wanted)
+    for s in range(HEAVY):
+        request = jnp.where(lane == devices + s, total_of(marked & (rank == s), panel_slot(lane), 1), request)
+    heavy_hit = hit_down & marked_down
+    local = cols & (blocks - 1)
+    slot = jnp.where(
+        total_of(heavy_hit, 1, 0) > 0,
+        devices + ((local & (PLANE - 1)) * 2 + (local >> 3)) * HEAVY + total_of(heavy_hit, jnp.broadcast_to(rank_down, i.shape), 0),
+        panel_slot(cols >> shift),
+    )
+    slot = jnp.where((cols >> shift) == me, devices + HEAVY * blocks + local, slot)
+    side = counts.shape[1]
+    ends = total_of(j[:side, :side] <= i[:side, :side], jnp.broadcast_to(counts, (side, side)), 1)
+    row = total_of(ends <= j[:side], 1, 0)
+    return request, slot, row
+
+
+def exchange_kernel(cols, counts, features, arrived_out, heavy_out, plan_out, *scratch):
     names = ("own", "up1", "down1", "up2", "down2", "up3s", "down3s", "up3", "down3", "far", "picked", "arrived", "gathered")
     bufs = {n: scratch[i * PARTS : (i + 1) * PARTS] for i, n in enumerate(names)}
     own, up1, down1, up2, down2, up3s, down3s, up3, down3, far, picked, arrived, gathered = (bufs[n] for n in names)
-    load_sem, zs, zr, xs, xr, gs, gr, out_sem = scratch[len(names) * PARTS :]
+    (rows_buf, table, load_sem, zs, zr, xs, xr, gs, gr, out_sem, ps, pr, table_sem) = scratch[len(names) * PARTS :]
     me = lax.axis_index("rows")
     z, q = me // PLANE, lax.rem(me, PLANE)
     x, c = q // 2, lax.rem(q, 2)
@@ -129,7 +173,8 @@
     for k in range(PARTS):
         load(k).start()
     barrier = pltpu.get_barrier_semaphore()
-    for peer in (up, down):
+    second_up, second_down = at(2) * PLANE + q, at(-2) * PLANE + q
+    for peer in (up, down, second_up, second_down):
         pl.semaphore_signal(barrier, inc=1, device_id={"rows": peer}, device_id_type=MESH)
 
     @pl.loop(1, PLANE)
@@ -137,7 +182,7 @@
         peer = z * PLANE + lax.rem(q + p, PLANE)
         pl.semaphore_signal(barrier, inc=1, device_id={"rows": peer}, device_id_type=MESH)
 
-    pl.semaphore_wait(barrier, PLANE + 1)
+    pl.semaphore_wait(barrier, PLANE + 3)
 
     def send(src, dst, ssem, rsem, peer):
         return pltpu.make_async_remote_copy(
@@ -166,7 +211,45 @@
             copy.wait_recv()
 
     def block_of(dz_reader, reader, dz_owner):
-        return table[(at(dz_reader) * PLANE + reader) * (PLANES * PLANE) + at(dz_owner) * PLANE + q]
+        return table[at(dz_reader) * PLANE + reader, 0, at(dz_owner) * PLANE + q]
+
+    def plane_rows(dz):
+        return pl.ds(at(dz) * PLANE, PLANE)
+
+    def table_copy(i, dz):
+        return pltpu.make_async_copy(rows_buf.at[plane_rows(dz)], table.at[plane_rows(dz)], table_sem.at[i])
+
+    hops = ((up, -1), (down, 1), (second_up, -2), (second_down, 2))
+
+    def rows_copy(i):
+        src = rows_buf.at[plane_rows(0)]
+        return send(src, src, ps.at[1 + i], pr.at[1 + i], hops[i][0])
+
+    def share_plan():
+        request, slot, row = plan_rows(me, cols[...], counts[...], own[0].shape[0])
+        plan_out[0:1] = slot
+        plan_out[1:2] = row
+        rows_buf[me] = request
+
+        @pl.loop(1, PLANE)
+        def _(p):
+            src = rows_buf.at[me]
+            send(src, src, ps.at[0], pr.at[0], z * PLANE + lax.rem(q + p, PLANE)).start()
+
+        most = rows_buf.at[pl.ds(0, PLANE - 1)]
+        pltpu.make_async_copy(most, most, pr.at[0]).wait()
+        for i in range(4):
+            rows_copy(i).start()
+        table_copy(0, 0).start()
+        table_copy(0, 0).wait()
+
+    def take_plan():
+        for i, (_, dz) in enumerate(hops):
+            src = rows_buf.at[plane_rows(dz)]
+            pltpu.make_async_copy(src, src, pr.at[1 + i]).wait()
+            table_copy(1 + i, dz).start()
+        for i, (_, dz) in enumerate(hops):
+            table_copy(1 + i, dz).wait()
 
     def x_pick(k, first, sources):
         @pl.loop(0, PLANE)
@@ -237,6 +320,8 @@
         if s == 0:
             load(k).wait()
             z_start(k, 0)
+            if k == 0:
+                share_plan()
             x_pick(k, 0, [(own[k], 0)])
         elif s == 1:
             z_wait(k, 0)
@@ -244,6 +329,8 @@
             x_pick(k, 1, [(up1[k], -1), (down1[k], 1)])
         elif s == 2:
             z_wait(k, 1)
+            if k == 0:
+                take_plan()
 
             @pl.loop(0, PLANE)
             def _(reader):
@@ -270,7 +357,7 @@
             pltpu.make_async_copy(everything, everything, xr.at[k]).wait()
             arrived_store(k).start()
             for i in range(HEAVY):
-                gathered[k][q, 1 - even, i] = arrived[k][heavy_slot[i]]
+                gathered[k][q, 1 - even, i] = arrived[k][table[me, 0, PLANES * PLANE + i]]
             gather_copies(k, 0).start()
         elif s == 6:
             gather_copies(k, 0).wait_recv()
@@ -296,6 +383,10 @@
             if 0 <= t - s < PARTS:
                 stage(t - s, s)
 
+    most = rows_buf.at[pl.ds(0, PLANE - 1)]
+    pltpu.make_async_copy(most, most, ps.at[0]).wait()
+    for i in range(4):
+        rows_copy(i).wait_send()
     for k in range(PARTS):
         for step in range(4):
             for copy in z_copies(k, step):
@@ -309,10 +400,10 @@
         heavy_store(k).wait()
 
 
-def exchange(table, heavy_slot, own):
+def exchange(cols, counts, own):
     blocks, side, feat = own.shape
     rows = side // PARTS
-    smem = pl.BlockSpec(memory_space=pltpu.SMEM)
+    vmem = pl.BlockSpec(memory_space=pltpu.VMEM)
     anywhere = pl.BlockSpec(memory_space=pl.ANY)
     leads = [(blocks,)] * 5 + [(PLANE + 4,)] * 4 + [(2, 4), (PLANE, 5), (PLANE * PLANES,), (PLANE, 2, HEAVY)]
     bufs = [pltpu.VMEM(lead + (rows, feat), jnp.float32) for lead in leads for _ in range(PARTS)]
@@ -322,11 +413,14 @@
         out_shape=[
             jax.ShapeDtypeStruct((PARTS, PLANE * PLANES, rows, feat), jnp.float32),
             jax.ShapeDtypeStruct((PARTS, PLANE, 2, HEAVY, rows, feat), jnp.float32),
+            jax.ShapeDtypeStruct((2, cols.shape[1]), jnp.int32),
         ],
-        in_specs=[smem, smem, anywhere],
-        out_specs=[anywhere, anywhere],
+        in_specs=[vmem, vmem, anywhere],
+        out_specs=[anywhere, anywhere, vmem],
         scratch_shapes=bufs
         + [
+            pltpu.VMEM((PLANE * PLANES, 1, cols.shape[1]), jnp.int32),
+            pltpu.SMEM((PLANE * PLANES, 1, cols.shape[1]), jnp.int32),
             dma((PARTS,)),
             dma((PARTS * 8,)),
             dma((PARTS * 8,)),
@@ -335,9 +429,12 @@
             dma((PARTS * 9,)),
             dma((PARTS * 9,)),
             dma((PARTS * 2,)),
+            dma((5,)),
+            dma((5,)),
+            dma((5,)),
         ],
         compiler_params=pltpu.CompilerParams(collective_id=0, has_side_effects=True, vmem_limit_bytes=56 << 20),
-    )(table, heavy_slot, own)
+    )(cols, counts, own)
 
 
 def per_device(features, norm_gain, row_counts, tile_cols, tile_values):
@@ -345,49 +442,10 @@
     side = tile_values.shape[1]
     blocks = node_dev // side
     total = tile_values.shape[0]
-    devices = lax.axis_size("rows")
-    me = lax.axis_index("rows")
     own = features.reshape(blocks, side, feat_dev)
-    peers = jnp.arange(devices, dtype=jnp.int32)
-    owner = tile_cols // blocks
-    local = tile_cols % blocks
-    hit = owner[None, :] == peers[:, None]
-    wanted = jnp.max(jnp.where(hit, local[None, :], 0), axis=1)
-    marked = (jnp.sum(hit.astype(jnp.int32), axis=1) >= 2) & (peers != me)
-    i_am_heavy = jnp.sum(marked.astype(jnp.int32)) < HEAVY
-    marked = marked | ((peers == me) & i_am_heavy)
-    rank = jnp.sum((marked[None, :] & (peers[None, :] < peers[:, None])).astype(jnp.int32), axis=1)
-    ranks = jnp.arange(HEAVY, dtype=jnp.int32)
-    heavy_ids = jnp.sum(
-        jnp.where(marked[None, :] & (rank[None, :] == ranks[:, None]), peers[None, :], 0), axis=1
-    )
-    wanted = jnp.where(marked | (peers == me), me % GROUP, wanted)
-    table = lax.all_gather(wanted, "rows", axis=0, tiled=True)
-
-    def panel_slot(stripe):
-        ahead = (stripe // PLANE - me // PLANE + PLANES) % PLANES
-        return stripe % PLANE * PLANES + jnp.where(ahead < 4, 2 * ahead, 2 * (PLANES - ahead) - 1)
-
-    arrived, heavy = exchange(table, panel_slot(heavy_ids), own)
+    arrived, heavy, plan = exchange(tile_cols.reshape(1, total), row_counts, own)
     heavy = heavy.reshape((PARTS, blocks * HEAVY) + heavy.shape[-2:])
-    match = owner[:, None] == heavy_ids[None, :]
-    tile_rank = jnp.sum(match.astype(jnp.int32) * ranks[None, :], axis=1)
-    slot = jnp.where(
-        owner == me,
-        devices + HEAVY * blocks + local,
-        jnp.where(
-            jnp.any(match, axis=1),
-            devices + (local % PLANE * 2 + local // PLANE) * HEAVY + tile_rank,
-            panel_slot(owner),
-        ),
-    )
-    block_ids = jnp.arange(blocks, dtype=jnp.int32)
-    row_ends = jnp.sum(
-        jnp.where(block_ids[None, :] <= block_ids[:, None], row_counts[0][None, :], 0), axis=1
-    )
-    tile_index = jnp.arange(total, dtype=jnp.int32)
-    row = jnp.sum((row_ends[None, :] <= tile_index[:, None]).astype(jnp.int32), axis=1)
-    aggregate = tile_product(slot, row, tile_values, arrived, heavy, own)
+    aggregate = tile_product(plan, tile_values, arrived, heavy, own)
     aggregate = aggregate.reshape(node_dev, feat_dev)
     square_sum = lax.psum(jnp.sum(aggregate * aggregate, axis=1), "feat")
     mean_square = square_sum / (feat_dev * lax.axis_size("feat"))

time: 484 us -> 233 us (0.48)
  blocking collectives: 258 us -> 8.84 us
  Pallas kernels: 213 us -> 218 us
    unnamed x1 -> x0, blocking collectives: 249 us -> none
    pallas_call x1, Pallas kernels: 179 us -> 185 us  [exchange(): pl.pallas_call(exchange_kernel, out_shape=[jax.ShapeDtypeStruct((PARTS, P...]
where the time goes in v4:
time: 233 us; the launch traced here: 232 us
  Pallas kernels  218 us (94%)
  blocking collectives  8.84 us (4%)
  local copies, waits for them, and re-layouts  3.45 us (1%)
    pallas_call x1, Pallas kernels, exchange(): pl.pallas_call(exchange_kernel, out_shape=[jax.ShapeDtypeStruct((PARTS, P...  185 us
    pallas_call x1, Pallas kernels, tile_product(): pl.pallas_call(tile_kernel, out_shape=jax.ShapeDtypeStruct((blocks, side,...  32.8 us
    psum x1, blocking collectives, per_device(): square_sum = lax.psum(jnp.sum(aggregate * aggregate, axis=1), 'feat')  8.84 us

profile of v4, /device:TPU:1, one launch (start us, length us, event | category | flops | bytes accessed | tf_op | source)
XLA Modules:
  0.0 232.5 jit_solution(11858607447693740741)
XLA Ops:
  0.0 0.0 copy-start
  0.0 185.3 %shard_map.55 = (f32[4,64,32,256]{3,2,1,0:T(8,128)}, f32[4,8,2,3,32,256]{5,4,3,2,1,0:T(8,128)}, s32[2,128]{1,0:T(2,128)}) custom-call(s32[1,128]{1,0:T(1,128)} %bitcast.13, s32[1,16]{1,0:T(1,128)} %counts.1, f32[16,128,256]{2,1,0:T(8,128)} %bitcast.9), custom_call_target="tpu_custom_call" | custom-call | tf_op jit(solution)/shard_map/pallas_call | solution.py:411
  185.3 0.0 copy-done
  185.3 0.0 copy-start.1
  185.3 2.8 %copy-done.1 = f32[4,8,2,3,32,256]{5,4,3,2,1,0:T(8,128)S(1)} copy-done((f32[4,8,2,3,32,256]{5,4,3,2,1,0:T(8,128)S(1)}, f32[4,8,2,3,32,256]{5,4,3,2,1,0:T(8,128)}, u32[]{:S(2)}) %copy-start.1) | copy-done | bytes 6291480
  188.1 0.0 copy-start.2
  188.1 0.7 copy-done.2
  188.8 32.8 %shard_map.56 = f32[16,128,256]{2,1,0:T(8,128)S(1)} custom-call(s32[2,128]{1,0:T(2,128)S(1)} %copy-done.2, f32[128,128,128]{2,1,0:T(8,128)} %tiles.1, f32[4,64,32,256]{3,2,1,0:T(8,128)} %get-tuple-element.9.arrived, f32[4,48,32,256]{3,2,1,0:T(8,128)S(1)} %bitcast.11, f32[16,4,32,256]{3,2,1,0:T(8,128)S(1)} %bitcast.10), custom_call_target="tpu_custom_call" | custom-call | tf_op jit(solution)/shard_map/pallas_call | solution.py:85
  221.6 0.0 copy-start.3
  221.6 0.3 multiply_reduce_fusion
  221.9 8.8 %psum.7 = f32[2048]{0:T(1024)S(1)} all-reduce(f32[2048]{0:T(1024)S(1)} %bitcast.12), channel_id=1, replica_groups=mesh['rows'=64,'feat'=4] {'feat'}, use_global_device_ids=true, to_apply=%region_1.0 | all-reduce | flops 2048 | bytes 16384 | tf_op jit(solution)/shard_map/psum | solution.py:450
  230.8 0.0 copy-done.3
  230.8 1.7 fusion
  (1 shorter events, 0.0 us)
Async XLA Ops:
  0.0 185.3 %copy-start = (f32[2048,256]{1,0:T(8,128)S(1)}, f32[2048,256]{1,0:T(8,128)}, u32[]{:S(2)}) copy-start(f32[2048,256]{1,0:T(8,128)} %param.5) | copy-start | bytes 6291460
  185.3 2.8 %copy-start.1 = (f32[4,8,2,3,32,256]{5,4,3,2,1,0:T(8,128)S(1)}, f32[4,8,2,3,32,256]{5,4,3,2,1,0:T(8,128)}, u32[]{:S(2)}) copy-start(f32[4,8,2,3,32,256]{5,4,3,2,1,0:T(8,128)} %get-tuple-element.10) | copy-start | bytes 18874372
  188.1 0.7 copy-start.2
  221.6 9.2 %copy-start.3 = (f32[256]{0:T(256)S(1)}, f32[256]{0:T(256)}, u32[]{:S(2)}) copy-start(f32[256]{0:T(256)} %param.6) | copy-start | bytes 3076

commit v5 on v4

--- a/solution.py
+++ b/solution.py
@@ -9,92 +9,51 @@
 
 HEAVY = 3
 GROUP = 16
-DEPTH = 16
-CHUNK = 8
-
-
-def tile_kernel(plan, tiles, arrived, heavy, own, out, abuf, xbuf, asem, xsem):
-    total = tiles.shape[0]
-    n_arr, n_heavy = arrived.shape[1], heavy.shape[1]
-    side, feat = own.shape[1] * own.shape[2], own.shape[3]
-
-    def tile_copy(c):
-        part = pl.ds(c * CHUNK, CHUNK)
-        return pltpu.make_async_copy(tiles.at[part], abuf.at[part], asem.at[c])
-
-    def fetch(t):
-        s, b = plan[0, t], lax.rem(t, DEPTH)
-
-        @pl.when(s < n_arr)
-        def _():
-            pltpu.make_async_copy(arrived.at[:, s], xbuf.at[b], xsem.at[b]).start()
-
-        @pl.when((s >= n_arr) & (s < n_arr + n_heavy))
-        def _():
-            pltpu.make_async_copy(heavy.at[:, s - n_arr], xbuf.at[b], xsem.at[b]).start()
-
-        @pl.when(s >= n_arr + n_heavy)
-        def _():
-            pltpu.make_async_copy(own.at[s - n_arr - n_heavy], xbuf.at[b], xsem.at[b]).start()
-
-    for c in range(2):
-        tile_copy(c).start()
-
-    @pl.loop(0, DEPTH)
-    def _(t):
-        fetch(t)
-
-    @pl.loop(2, total // CHUNK)
-    def _(c):
-        tile_copy(c).start()
-
+TOGETHER = 4
+
+
+def halves(value):
+    high = value.astype(jnp.bfloat16)
+    return high, (value - high.astype(jnp.float32)).astype(jnp.bfloat16)
+
+
+def tile_kernel(plan, tiles, *rest):
+    panel, heavy = rest[:PARTS], rest[PARTS : 2 * PARTS]
+    out = rest[2 * PARTS]
+    total, light = tiles.shape[0], panel[0].shape[0]
     out[...] = jnp.zeros_like(out)
 
-    @pl.loop(0, total)
-    def _(t):
-        b = lax.rem(t, DEPTH)
-
-        @pl.when(lax.rem(t, CHUNK) == 0)
-        def _():
-            tile_copy(t // CHUNK).wait()
-
-        pltpu.make_async_copy(arrived.at[:, 0], xbuf.at[b], xsem.at[b]).wait()
-        a = abuf[t]
-        x = jnp.maximum(xbuf[b].reshape(side, feat), 0.0)
-        a_hi = a.astype(jnp.bfloat16)
-        a_lo = (a - a_hi.astype(jnp.float32)).astype(jnp.bfloat16)
-        x_hi = x.astype(jnp.bfloat16)
-        x_lo = (x - x_hi.astype(jnp.float32)).astype(jnp.bfloat16)
-        prod = jnp.dot(
+    def product(t):
+        slot = plan[0, t]
+        is_light, i, j = slot < light, jnp.minimum(slot, light - 1), jnp.maximum(slot - light, 0)
+        x = jnp.concatenate([jnp.where(is_light, panel[k][i], heavy[k][j]) for k in range(PARTS)], axis=0)
+        x_hi, x_lo = halves(jnp.maximum(x, 0.0))
+        a_hi, a_lo = halves(tiles[t])
+        return jnp.dot(
             jnp.concatenate([a_hi, a_lo], axis=1),
             jnp.concatenate([x_hi, x_hi], axis=0),
             preferred_element_type=jnp.float32,
         ) + jnp.dot(a_hi, x_lo, preferred_element_type=jnp.float32)
-        out[plan[1, t]] += prod
-
-        @pl.when(t + DEPTH < total)
-        def _():
-            fetch(t + DEPTH)
-
-
-def tile_product(plan, tiles, arrived, heavy, own):
-    blocks, side, feat = own.shape
-    total = tiles.shape[0]
-    smem = pl.BlockSpec(memory_space=pltpu.SMEM)
-    anywhere = pl.BlockSpec(memory_space=pl.ANY)
+
+    @pl.loop(0, total // TOGETHER)
+    def _(step):
+        ts = [step * TOGETHER + u for u in range(TOGETHER)]
+        products = [product(t) for t in ts]
+        for t, prod in zip(ts, products):
+            out[plan[1, t]] += prod
+
+
+def tile_product(plan, tiles, panel, heavy):
+    side = tiles.shape[1]
+    blocks, feat = panel[0].shape[0] - PLANE * PLANES, panel[0].shape[-1]
+    vmem = pl.BlockSpec(memory_space=pltpu.VMEM)
     return pl.pallas_call(
         tile_kernel,
         out_shape=jax.ShapeDtypeStruct((blocks, side, feat), jnp.float32),
-        in_specs=[smem, anywhere, anywhere, anywhere, anywhere],
-        out_specs=pl.BlockSpec(memory_space=pltpu.VMEM),
-        scratch_shapes=[
-            pltpu.VMEM(tiles.shape, jnp.float32),
-            pltpu.VMEM((DEPTH, PARTS, side // PARTS, feat), jnp.float32),
-            pltpu.SemaphoreType.DMA((total // CHUNK,)),
-            pltpu.SemaphoreType.DMA((DEPTH,)),
-        ],
-        compiler_params=pltpu.CompilerParams(vmem_limit_bytes=40 << 20),
-    )(plan, tiles, arrived, heavy, own.reshape(blocks, PARTS, side // PARTS, feat))
+        in_specs=[pl.BlockSpec(memory_space=pltpu.SMEM)] + [vmem] * (2 * PARTS + 1),
+        out_specs=vmem,
+        compiler_params=pltpu.CompilerParams(vmem_limit_bytes=8 << 20),
+    )(plan, tiles, *panel, *heavy)
 
 
 PARTS = 4
@@ -137,21 +96,23 @@
     local = cols & (blocks - 1)
     slot = jnp.where(
         total_of(heavy_hit, 1, 0) > 0,
-        devices + ((local & (PLANE - 1)) * 2 + (local >> 3)) * HEAVY + total_of(heavy_hit, jnp.broadcast_to(rank_down, i.shape), 0),
+        devices + blocks + ((local & (PLANE - 1)) * 2 + (local >> 3)) * HEAVY + total_of(heavy_hit, jnp.broadcast_to(rank_down, i.shape), 0),
         panel_slot(cols >> shift),
     )
-    slot = jnp.where((cols >> shift) == me, devices + HEAVY * blocks + local, slot)
+    slot = jnp.where((cols >> shift) == me, devices + local, slot)
     side = counts.shape[1]
     ends = total_of(j[:side, :side] <= i[:side, :side], jnp.broadcast_to(counts, (side, side)), 1)
     row = total_of(ends <= j[:side], 1, 0)
     return request, slot, row
 
 
-def exchange_kernel(cols, counts, features, arrived_out, heavy_out, plan_out, *scratch):
-    names = ("own", "up1", "down1", "up2", "down2", "up3s", "down3s", "up3", "down3", "far", "picked", "arrived", "gathered")
+def exchange_kernel(cols, counts, features, tiles, *rest):
+    arrived, gathered = rest[:PARTS], rest[PARTS : 2 * PARTS]
+    plan_out, tiles_out, scratch = rest[2 * PARTS], rest[2 * PARTS + 1], rest[2 * PARTS + 2 :]
+    names = ("own", "up1", "down1", "up2", "down2", "up3s", "down3s", "up3", "down3", "far", "picked")
     bufs = {n: scratch[i * PARTS : (i + 1) * PARTS] for i, n in enumerate(names)}
-    own, up1, down1, up2, down2, up3s, down3s, up3, down3, far, picked, arrived, gathered = (bufs[n] for n in names)
-    (rows_buf, table, load_sem, zs, zr, xs, xr, gs, gr, out_sem, ps, pr, table_sem) = scratch[len(names) * PARTS :]
+    own, up1, down1, up2, down2, up3s, down3s, up3, down3, far, picked = (bufs[n] for n in names)
+    (rows_buf, table, load_sem, zs, zr, xs, xr, gs, gr, out_sem, ps, pr, table_sem, tile_sem) = scratch[len(names) * PARTS :]
     me = lax.axis_index("rows")
     z, q = me // PLANE, lax.rem(me, PLANE)
     x, c = q // 2, lax.rem(q, 2)
@@ -172,6 +133,8 @@
 
     for k in range(PARTS):
         load(k).start()
+    tile_load = pltpu.make_async_copy(tiles, tiles_out, tile_sem)
+    tile_load.start()
     barrier = pltpu.get_barrier_semaphore()
     second_up, second_down = at(2) * PLANE + q, at(-2) * PLANE + q
     for peer in (up, down, second_up, second_down):
@@ -310,16 +273,15 @@
         j = PARTS * 8 + k
         return send(src, src, gs.at[j], gr.at[j], other)
 
-    def arrived_store(k):
-        return pltpu.make_async_copy(arrived[k], arrived_out.at[k], out_sem.at[k])
-
-    def heavy_store(k):
-        return pltpu.make_async_copy(gathered[k], heavy_out.at[k], out_sem.at[PARTS + k])
+    def keep_own(k):
+        part = pl.ds(PLANE * PLANES, own[k].shape[0])
+        return pltpu.make_async_copy(features.at[:, pl.ds(k * part_rows, part_rows)], arrived[k].at[part], out_sem.at[k])
 
     def stage(k, s):
         if s == 0:
             load(k).wait()
             z_start(k, 0)
+            keep_own(k).start()
             if k == 0:
                 share_plan()
             x_pick(k, 0, [(own[k], 0)])
@@ -355,7 +317,7 @@
         elif s == 5:
             everything = arrived[k].at[pl.ds(0, (PLANE - 1) * PLANES)]
             pltpu.make_async_copy(everything, everything, xr.at[k]).wait()
-            arrived_store(k).start()
+            keep_own(k).wait()
             for i in range(HEAVY):
                 gathered[k][q, 1 - even, i] = arrived[k][table[me, 0, PLANES * PLANE + i]]
             gather_copies(k, 0).start()
@@ -376,13 +338,13 @@
             for i in (5, 6, 7):
                 gather_copies(k, i).wait_recv()
             last_core_copy(k).wait_recv()
-            heavy_store(k).start()
 
     for t in range(PARTS + 9):
         for s in range(10):
             if 0 <= t - s < PARTS:
                 stage(t - s, s)
 
+    tile_load.wait()
     most = rows_buf.at[pl.ds(0, PLANE - 1)]
     pltpu.make_async_copy(most, most, ps.at[0]).wait()
     for i in range(4):
@@ -396,27 +358,23 @@
         for i in range(8):
             gather_copies(k, i).wait_send()
         last_core_copy(k).wait_send()
-        arrived_store(k).wait()
-        heavy_store(k).wait()
-
-
-def exchange(cols, counts, own):
+
+
+def exchange(cols, counts, own, tiles):
     blocks, side, feat = own.shape
     rows = side // PARTS
     vmem = pl.BlockSpec(memory_space=pltpu.VMEM)
     anywhere = pl.BlockSpec(memory_space=pl.ANY)
-    leads = [(blocks,)] * 5 + [(PLANE + 4,)] * 4 + [(2, 4), (PLANE, 5), (PLANE * PLANES,), (PLANE, 2, HEAVY)]
+    leads = [(blocks,)] * 5 + [(PLANE + 4,)] * 4 + [(2, 4), (PLANE, 5)]
     bufs = [pltpu.VMEM(lead + (rows, feat), jnp.float32) for lead in leads for _ in range(PARTS)]
     dma = pltpu.SemaphoreType.DMA
     return pl.pallas_call(
         exchange_kernel,
-        out_shape=[
-            jax.ShapeDtypeStruct((PARTS, PLANE * PLANES, rows, feat), jnp.float32),
-            jax.ShapeDtypeStruct((PARTS, PLANE, 2, HEAVY, rows, feat), jnp.float32),
-            jax.ShapeDtypeStruct((2, cols.shape[1]), jnp.int32),
-        ],
-        in_specs=[vmem, vmem, anywhere],
-        out_specs=[anywhere, anywhere, vmem],
+        out_shape=[jax.ShapeDtypeStruct((PLANE * PLANES + blocks, rows, feat), jnp.float32)] * PARTS
+        + [jax.ShapeDtypeStruct((PLANE, 2, HEAVY, rows, feat), jnp.float32)] * PARTS
+        + [jax.ShapeDtypeStruct((2, cols.shape[1]), jnp.int32), jax.ShapeDtypeStruct(tiles.shape, jnp.float32)],
+        in_specs=[vmem, vmem, anywhere, anywhere],
+        out_specs=[vmem] * (2 * PARTS + 2),
         scratch_shapes=bufs
         + [
             pltpu.VMEM((PLANE * PLANES, 1, cols.shape[1]), jnp.int32),
@@ -428,13 +386,14 @@
             dma((PARTS,)),
             dma((PARTS * 9,)),
             dma((PARTS * 9,)),
-            dma((PARTS * 2,)),
+            dma((PARTS,)),
             dma((5,)),
             dma((5,)),
             dma((5,)),
+            dma,
         ],
-        compiler_params=pltpu.CompilerParams(collective_id=0, has_side_effects=True, vmem_limit_bytes=56 << 20),
-    )(cols, counts, own)
+        compiler_params=pltpu.CompilerParams(collective_id=0, has_side_effects=True, vmem_limit_bytes=25 << 20),
+    )(cols, counts, own, tiles)
 
 
 def per_device(features, norm_gain, row_counts, tile_cols, tile_values):
@@ -443,9 +402,9 @@
     blocks = node_dev // side
     total = tile_values.shape[0]
     own = features.reshape(blocks, side, feat_dev)
-    arrived, heavy, plan = exchange(tile_cols.reshape(1, total), row_counts, own)
-    heavy = heavy.reshape((PARTS, blocks * HEAVY) + heavy.shape[-2:])
-    aggregate = tile_product(plan, tile_values, arrived, heavy, own)
+    *blocks_got, plan, tiles = exchange(tile_cols.reshape(1, total), row_counts, own, tile_values)
+    panel, heavy = blocks_got[:PARTS], [h.reshape((blocks * HEAVY,) + h.shape[-2:]) for h in blocks_got[PARTS:]]
+    aggregate = tile_product(plan, tiles, panel, heavy)
     aggregate = aggregate.reshape(node_dev, feat_dev)
     square_sum = lax.psum(jnp.sum(aggregate * aggregate, axis=1), "feat")
     mean_square = square_sum / (feat_dev * lax.axis_size("feat"))

time: 233 us -> 209 us (0.90)
  Pallas kernels: 218 us -> 195 us
    pallas_call x1, Pallas kernels: 32.8 us -> 11.7 us  [tile_product(): pl.pallas_call(tile_kernel, out_shape=jax.ShapeDtypeStruct((blocks, side,...]
where the time goes in v5:
time: 209 us
  Pallas kernels  195 us (93%)
  blocking collectives  8.84 us (4%)
  local copies, waits for them, and re-layouts  2.91 us (1%)
    pallas_call x1, Pallas kernels, exchange(): pl.pallas_call(exchange_kernel, out_shape=[jax.ShapeDtypeStruct((PLANE *...  183 us
    pallas_call x1, Pallas kernels, tile_product(): pl.pallas_call(tile_kernel, out_shape=jax.ShapeDtypeStruct((blocks, side,...  11.7 us
    psum x1, blocking collectives, per_device(): square_sum = lax.psum(jnp.sum(aggregate * aggregate, axis=1), 'feat')  8.84 us

profile of v5, /device:TPU:1, one launch (start us, length us, event | category | flops | bytes accessed | tf_op | source)
XLA Modules:
  0.0 208.6 jit_solution(14635819758808315164)
XLA Ops:
  0.0 0.0 copy-start
  0.0 1.6 copy-done
  1.6 0.0 copy-start.1
  1.6 0.7 copy-done.1
  2.2 0.0 copy-start.2
  2.2 0.7 copy-done.2
  2.9 183.1 %shard_map.55 = (f32[80,32,256]{2,1,0:T(8,128)S(1)}, f32[80,32,256]{2,1,0:T(8,128)S(1)}, f32[80,32,256]{2,1,0:T(8,128)S(1)}, f32[80,32,256]{2,1,0:T(8,128)S(1)},...) custom-call(s32[1,128]{1,0:T(1,128)S(1)} %bitcast.16, ...), custom_call_target="tpu_custom_call" | custom-call | tf_op jit(solution)/shard_map/pallas_call | solution.py:371
  186.0 11.7 %shard_map.56 = f32[16,128,256]{2,1,0:T(8,128)S(1)} custom-call(s32[2,128]{1,0:T(2,128)S(1)} %get-tuple-element.15.plan, f32[128,128,128]{2,1,0:T(8,128)S(1)} %get-tuple-element.16.tiles, f32[80,32,256]{2,1,0:T(8,128)S(1)} %get-tuple-element.17.rest_0_, f32[80,32,256]{2,1,0:T(8,128)S(1)} %get-tuple-element.18.rest_1_, ...), custom_call_target="tpu_custom_call" | custom-call | tf_op jit(solution)/shard_map/pallas_call | solution.py:50
  197.7 0.0 copy-start.3
  197.7 0.3 multiply_reduce_fusion
  198.1 8.8 %psum.7 = f32[2048]{0:T(1024)S(1)} all-reduce(f32[2048]{0:T(1024)S(1)} %bitcast.17), channel_id=1, replica_groups=mesh['rows'=64,'feat'=4] {'feat'}, use_global_device_ids=true, to_apply=%region_1.0 | all-reduce | flops 2048 | bytes 16384 | tf_op jit(solution)/shard_map/psum | solution.py:409
  206.9 0.0 copy-done.3
  207.0 1.7 fusion
  (1 shorter events, 0.0 us)
Async XLA Ops:
  0.0 1.6 copy-start
  1.6 0.7 copy-start.1
  2.2 0.7 copy-start.2
  197.7 9.2 %copy-start.3 = (f32[256]{0:T(256)S(1)}, f32[256]{0:T(256)}, u32[]{:S(2)}) copy-start(f32[256]{0:T(256)} %param.6) | copy-start | bytes 3076

commit v6 on v5

--- a/solution.py
+++ b/solution.py
@@ -56,9 +56,10 @@
     )(plan, tiles, *panel, *heavy)
 
 
-PARTS = 4
+PARTS = 8
 PLANE = 8
 PLANES = 8
+ORDER = ((0, 0), (1, 1), (2, 2), (3, 3), (4, 4), (5, 5), (6, 6), (7, 7), (8, 8), (9, 9))
 MESH = pl.DeviceIdType.MESH
 
 
@@ -112,7 +113,7 @@
     names = ("own", "up1", "down1", "up2", "down2", "up3s", "down3s", "up3", "down3", "far", "picked")
     bufs = {n: scratch[i * PARTS : (i + 1) * PARTS] for i, n in enumerate(names)}
     own, up1, down1, up2, down2, up3s, down3s, up3, down3, far, picked = (bufs[n] for n in names)
-    (rows_buf, table, load_sem, zs, zr, xs, xr, gs, gr, out_sem, ps, pr, table_sem, tile_sem) = scratch[len(names) * PARTS :]
+    (rows_buf, table, load_sem, zs, zr, xs, xr, gs, gr, out_sem, ps, pr, table_sem, tile_sem, cols_buf, counts_buf, small_sem) = scratch[len(names) * PARTS :]
     me = lax.axis_index("rows")
     z, q = me // PLANE, lax.rem(me, PLANE)
     x, c = q // 2, lax.rem(q, 2)
@@ -133,6 +134,12 @@
 
     for k in range(PARTS):
         load(k).start()
+    small_loads = (
+        pltpu.make_async_copy(cols, cols_buf, small_sem.at[0]),
+        pltpu.make_async_copy(counts, counts_buf, small_sem.at[1]),
+    )
+    for copy in small_loads:
+        copy.start()
     tile_load = pltpu.make_async_copy(tiles, tiles_out, tile_sem)
     tile_load.start()
     barrier = pltpu.get_barrier_semaphore()
@@ -189,7 +196,9 @@
         return send(src, src, ps.at[1 + i], pr.at[1 + i], hops[i][0])
 
     def share_plan():
-        request, slot, row = plan_rows(me, cols[...], counts[...], own[0].shape[0])
+        for copy in small_loads:
+            copy.wait()
+        request, slot, row = plan_rows(me, cols_buf[...], counts_buf[...], own[0].shape[0])
         plan_out[0:1] = slot
         plan_out[1:2] = row
         rows_buf[me] = request
@@ -340,9 +349,9 @@
             last_core_copy(k).wait_recv()
 
     for t in range(PARTS + 9):
-        for s in range(10):
-            if 0 <= t - s < PARTS:
-                stage(t - s, s)
+        for s, lag in ORDER:
+            if 0 <= t - lag < PARTS:
+                stage(t - lag, s)
 
     tile_load.wait()
     most = rows_buf.at[pl.ds(0, PLANE - 1)]
@@ -364,7 +373,7 @@
     blocks, side, feat = own.shape
     rows = side // PARTS
     vmem = pl.BlockSpec(memory_space=pltpu.VMEM)
-    anywhere = pl.BlockSpec(memory_space=pl.ANY)
+    hbm = pl.BlockSpec(memory_space=pltpu.HBM)
     leads = [(blocks,)] * 5 + [(PLANE + 4,)] * 4 + [(2, 4), (PLANE, 5)]
     bufs = [pltpu.VMEM(lead + (rows, feat), jnp.float32) for lead in leads for _ in range(PARTS)]
     dma = pltpu.SemaphoreType.DMA
@@ -373,7 +382,7 @@
         out_shape=[jax.ShapeDtypeStruct((PLANE * PLANES + blocks, rows, feat), jnp.float32)] * PARTS
         + [jax.ShapeDtypeStruct((PLANE, 2, HEAVY, rows, feat), jnp.float32)] * PARTS
         + [jax.ShapeDtypeStruct((2, cols.shape[1]), jnp.int32), jax.ShapeDtypeStruct(tiles.shape, jnp.float32)],
-        in_specs=[vmem, vmem, anywhere, anywhere],
+        in_specs=[hbm] * 4,
         out_specs=[vmem] * (2 * PARTS + 2),
         scratch_shapes=bufs
         + [
@@ -391,9 +400,55 @@
             dma((5,)),
             dma((5,)),
             dma,
+            pltpu.VMEM(cols.shape, jnp.int32),
+            pltpu.VMEM(counts.shape, jnp.int32),
+            dma((2,)),
         ],
         compiler_params=pltpu.CompilerParams(collective_id=0, has_side_effects=True, vmem_limit_bytes=25 << 20),
     )(cols, counts, own, tiles)
+
+
+def feat_sum_kernel(share, out, held, ss, rs):
+    me, size = lax.axis_index("feat"), held.shape[0]
+    peers = [lax.rem(me + p, size) for p in range(1, size)]
+    barrier = pltpu.get_barrier_semaphore()
+    for peer in peers:
+        pl.semaphore_signal(barrier, inc=1, device_id={"feat": peer}, device_id_type=MESH)
+    held[me] = share[...]
+    pl.semaphore_wait(barrier, size - 1)
+    copies = [
+        pltpu.make_async_remote_copy(
+            src_ref=held.at[me],
+            dst_ref=held.at[me],
+            send_sem=ss.at[i],
+            recv_sem=rs.at[i],
+            device_id={"feat": peer},
+            device_id_type=MESH,
+        )
+        for i, peer in enumerate(peers)
+    ]
+    for copy in copies:
+        copy.start()
+    for copy in copies:
+        copy.wait()
+    out[...] = sum(held[i] for i in range(size))
+
+
+def feat_sum(share):
+    size = lax.axis_size("feat")
+    vmem = pl.BlockSpec(memory_space=pltpu.VMEM)
+    return pl.pallas_call(
+        feat_sum_kernel,
+        out_shape=jax.ShapeDtypeStruct(share.shape, jnp.float32),
+        in_specs=[vmem],
+        out_specs=vmem,
+        scratch_shapes=[
+            pltpu.VMEM((size,) + share.shape, jnp.float32),
+            pltpu.SemaphoreType.DMA((size - 1,)),
+            pltpu.SemaphoreType.DMA((size - 1,)),
+        ],
+        compiler_params=pltpu.CompilerParams(collective_id=1, has_side_effects=True, vmem_limit_bytes=2 << 20),
+    )(share)
 
 
 def per_device(features, norm_gain, row_counts, tile_cols, tile_values):
@@ -405,10 +460,10 @@
     *blocks_got, plan, tiles = exchange(tile_cols.reshape(1, total), row_counts, own, tile_values)
     panel, heavy = blocks_got[:PARTS], [h.reshape((blocks * HEAVY,) + h.shape[-2:]) for h in blocks_got[PARTS:]]
     aggregate = tile_product(plan, tiles, panel, heavy)
-    aggregate = aggregate.reshape(node_dev, feat_dev)
-    square_sum = lax.psum(jnp.sum(aggregate * aggregate, axis=1), "feat")
+    square_sum = feat_sum(jnp.sum(aggregate * aggregate, axis=2))
     mean_square = square_sum / (feat_dev * lax.axis_size("feat"))
-    return aggregate * norm_gain[None, :] * lax.rsqrt(mean_square + 1e-05)[:, None]
+    normed = aggregate * norm_gain[None, None, :] * lax.rsqrt(mean_square + 1e-05)[:, :, None]
+    return normed.reshape(node_dev, feat_dev)
 
 
 def solution(mesh):

time: 209 us -> 198 us (0.947)
  blocking collectives: 8.84 us -> 0 us
    psum x1 -> x0, blocking collectives: 8.84 us -> none  [per_device(): square_sum = lax.psum(jnp.sum(aggregate * aggregate, axis=1), 'feat')]
    pallas_call x1, Pallas kernels: 183 us -> 175 us  [exchange(): pl.pallas_call(exchange_kernel, out_shape=[jax.ShapeDtypeStruct((PLANE *...]
    pallas_call x0 -> x1, Pallas kernels: none -> 5.27 us  [feat_sum(): pl.pallas_call(feat_sum_kernel, out_shape=jax.ShapeDtypeStruct(share.shap...]
where the time goes in v6:
time: 198 us
  Pallas kernels  193 us (97%)
  local copies, waits for them, and re-layouts  2.91 us (1%)
  other arithmetic  2.02 us (1%)
    pallas_call x1, Pallas kernels, exchange(): pl.pallas_call(exchange_kernel, out_shape=[jax.ShapeDtypeStruct((PLANE *...  175 us
    pallas_call x1, Pallas kernels, tile_product(): pl.pallas_call(tile_kernel, out_shape=jax.ShapeDtypeStruct((blocks, side,...  12 us
    pallas_call x1, Pallas kernels, feat_sum(): pl.pallas_call(feat_sum_kernel, out_shape=jax.ShapeDtypeStruct(share.shap...  5.27 us

profile of v6, /device:TPU:1, one launch (start us, length us, event | category | flops | bytes accessed | tf_op | source)
XLA Modules:
  0.0 197.7 jit_solution(5314318457657029500)
XLA Ops:
  0.0 0.0 copy-start
  0.0 1.6 copy-done
  1.6 0.0 copy-start.1
  1.6 0.7 copy-done.1
  2.2 0.0 copy-start.2
  2.2 0.7 copy-done.2
  2.9 175.4 %shard_map.55 = (f32[80,16,256]{2,1,0:T(8,128)S(1)}, f32[80,16,256]{2,1,0:T(8,128)S(1)}, f32[80,16,256]{2,1,0:T(8,128)S(1)}, f32[80,16,256]{2,1,0:T(8,128)S(1)},...) custom-call(s32[1,128]{1,0:T(1,128)S(1)} %bitcast.20, ...), custom_call_target="tpu_custom_call" | custom-call | tf_op jit(solution)/shard_map/pallas_call | solution.py:380
  178.3 12.0 %shard_map.56 = f32[16,128,256]{2,1,0:T(8,128)S(1)} custom-call(s32[2,128]{1,0:T(2,128)S(1)} %get-tuple-element.23.plan, f32[128,128,128]{2,1,0:T(8,128)S(1)} %get-tuple-element.24.tiles, f32[80,16,256]{2,1,0:T(8,128)S(1)} %get-tuple-element.25.rest_0_, f32[80,16,256]{2,1,0:T(8,128)S(1)} %get-tuple-element.26.rest_1_, ...), custom_call_target="tpu_custom_call" | custom-call | tf_op jit(solution)/shard_map/pallas_call | solution.py:50
  190.3 0.0 copy-start.3
  190.3 0.3 multiply_reduce_fusion.share
  190.7 5.3 %shard_map.57 = f32[16,128]{1,0:T(8,128)S(1)} custom-call(f32[16,128]{1,0:T(8,128)S(1)} %multiply_reduce_fusion.share), custom_call_target="tpu_custom_call" | custom-call | tf_op jit(solution)/shard_map/pallas_call | solution.py:440
  196.0 0.0 copy-done.3
  196.0 1.7 multiply_multiply_fusion
  (1 shorter events, 0.0 us)
Async XLA Ops:
  0.0 1.6 copy-start
  1.6 0.7 copy-start.1
  2.2 0.7 copy-start.2
  190.3 5.7 %copy-start.3 = (f32[256]{0:T(256)S(1)}, f32[256]{0:T(256)}, u32[]{:S(2)}) copy-start(f32[256]{0:T(256)} %param.6) | copy-start | bytes 3076

commit v7 on v6

--- a/solution.py
+++ b/solution.py
@@ -59,7 +59,7 @@
 PARTS = 8
 PLANE = 8
 PLANES = 8
-ORDER = ((0, 0), (1, 1), (2, 2), (3, 3), (4, 4), (5, 5), (6, 6), (7, 7), (8, 8), (9, 9))
+ORDER = tuple((stage, stage) for stage in range(10))
 MESH = pl.DeviceIdType.MESH
 
 
@@ -250,50 +250,49 @@
             reader = lax.rem(q + p, PLANE)
             send(source(reader), arrived[k].at[q * PLANES + first], xs.at[k], xr.at[k], z * PLANE + reader).start()
 
-    def gather_copy(k, i, src, dst, peer):
-        j = k * 8 + i
-        return send(src, dst, gs.at[j], gr.at[j], peer)
-
-    def mine(k, qq):
-        return gathered[k].at[qq]
-
     def q_of(xx):
         return lax.rem(x + xx + 4, 4) * 2 + c
 
-    def gather_copies(k, i):
-        if i == 0:
-            src = gathered[k].at[q, 1 - even]
-            return gather_copy(k, 0, src, src, partner)
-        if i == 1:
-            return gather_copy(k, 1, mine(k, q), mine(k, q), right)
-        if i == 2:
-            return gather_copy(k, 2, mine(k, q), mine(k, q), left)
-        if i == 3:
-            src = gathered[k].at[q_of(-1), 0]
-            return gather_copy(k, 3, src, src, right)
-        if i == 4:
-            src = gathered[k].at[q_of(1), 1]
-            return gather_copy(k, 4, src, src, left)
-        src = mine(k, q_of((0, 1, -1)[i - 5])) if i < 8 else None
-        return gather_copy(k, i, src, src, other)
-
-    def last_core_copy(k):
-        src = mine(k, q_of(2))
-        j = PARTS * 8 + k
-        return send(src, src, gs.at[j], gr.at[j], other)
+    def pieces_copy(k, i, qq, part, peer):
+        piece = gathered[k].at[qq, part]
+        return send(piece, piece, gs.at[k * 15 + i], gr.at[k * 15 + i], peer)
+
+    def to_partner(k):
+        return pieces_copy(k, 14, q, 1 - even, partner)
+
+    def over_x(k, p):
+        part = even if p else 1 - even
+        return [pieces_copy(k, p * 7 + i, q, part, peer) for i, peer in enumerate((right, left))]
+
+    def across(k, p):
+        return pieces_copy(k, p * 7 + 2, q_of(1 if p else -1), even if p else 1 - even, left if p else right)
+
+    def to_core(k, p):
+        part = even if p else 1 - even
+        return [pieces_copy(k, p * 7 + 3 + i, q_of(xx), part, other) for i, xx in enumerate((0, -1, 1, 2))]
 
     def keep_own(k):
         part = pl.ds(PLANE * PLANES, own[k].shape[0])
         return pltpu.make_async_copy(features.at[:, pl.ds(k * part_rows, part_rows)], arrived[k].at[part], out_sem.at[k])
 
+    def z_first(k):
+        load(k).wait()
+        z_start(k, 0)
+
     def stage(k, s):
         if s == 0:
-            load(k).wait()
-            z_start(k, 0)
-            keep_own(k).start()
             if k == 0:
+                z_first(0)
                 share_plan()
-            x_pick(k, 0, [(own[k], 0)])
+                for part in range(PARTS):
+                    if part == 1:
+                        z_first(1)
+                    elif part:
+                        load(part).wait()
+                    keep_own(part).start()
+                    x_pick(part, 0, [(own[part], 0)])
+            elif k > 1:
+                z_start(k, 0)
         elif s == 1:
             z_wait(k, 0)
             z_start(k, 1)
@@ -329,24 +328,29 @@
             keep_own(k).wait()
             for i in range(HEAVY):
                 gathered[k][q, 1 - even, i] = arrived[k][table[me, 0, PLANES * PLANE + i]]
-            gather_copies(k, 0).start()
+            for copy in [to_partner(k)] + over_x(k, 0) + to_core(k, 0)[:1]:
+                copy.start()
         elif s == 6:
-            gather_copies(k, 0).wait_recv()
-            for i in (1, 2, 5):
-                gather_copies(k, i).start()
+            to_partner(k).wait_recv()
+            for copy in over_x(k, 1) + to_core(k, 1)[:1]:
+                copy.start()
+            for came in over_x(k, 0):
+                came.wait_recv()
+            for copy in [across(k, 0)] + to_core(k, 0)[1:3]:
+                copy.start()
         elif s == 7:
-            gather_copies(k, 1).wait_recv()
-            gather_copies(k, 2).wait_recv()
-            for i in (3, 4, 6, 7):
-                gather_copies(k, i).start()
+            for came in over_x(k, 1):
+                came.wait_recv()
+            for copy in [across(k, 1)] + to_core(k, 1)[1:3]:
+                copy.start()
+            across(k, 0).wait_recv()
+            to_core(k, 0)[3].start()
         elif s == 8:
-            gather_copies(k, 3).wait_recv()
-            gather_copies(k, 4).wait_recv()
-            last_core_copy(k).start()
+            across(k, 1).wait_recv()
+            to_core(k, 1)[3].start()
         elif s == 9:
-            for i in (5, 6, 7):
-                gather_copies(k, i).wait_recv()
-            last_core_copy(k).wait_recv()
+            for copy in to_core(k, 0) + to_core(k, 1):
+                copy.wait_recv()
 
     for t in range(PARTS + 9):
         for s, lag in ORDER:
@@ -364,9 +368,8 @@
                 copy.wait_send()
         everything = arrived[k].at[pl.ds(0, (PLANE - 1) * PLANES)]
         pltpu.make_async_copy(everything, everything, xs.at[k]).wait()
-        for i in range(8):
-            gather_copies(k, i).wait_send()
-        last_core_copy(k).wait_send()
+        for copy in [to_partner(k)] + over_x(k, 0) + over_x(k, 1) + [across(k, 0), across(k, 1)] + to_core(k, 0) + to_core(k, 1):
+            copy.wait_send()
 
 
 def exchange(cols, counts, own, tiles):
@@ -393,8 +396,8 @@
             dma((PARTS * 8,)),
             dma((PARTS,)),
             dma((PARTS,)),
-            dma((PARTS * 9,)),
-            dma((PARTS * 9,)),
+            dma((PARTS * 15,)),
+            dma((PARTS * 15,)),
             dma((PARTS,)),
             dma((5,)),
             dma((5,)),
@@ -405,7 +408,7 @@
             dma((2,)),
         ],
         compiler_params=pltpu.CompilerParams(collective_id=0, has_side_effects=True, vmem_limit_bytes=25 << 20),
-    )(cols, counts, own, tiles)
+    )(*(pltpu.with_memory_space_constraint(a, pltpu.HBM) for a in (cols, counts, own, tiles)))
 
 
 def feat_sum_kernel(share, out, held, ss, rs):

time: 198 us -> 193 us (0.975)
  local copies, waits for them, and re-layouts: 2.91 us -> 0.01 us
  Pallas kernels: 193 us -> 191 us
    unnamed x8 -> x2, local copies, waits for them, and re-layouts: 2.91 us -> 0.01 us
where the time goes in v7:
time: 193 us
  Pallas kernels  191 us (99%)
  other arithmetic  2.02 us (1%)
    pallas_call x1, Pallas kernels, exchange(): pl.pallas_call(exchange_kernel, out_shape=[jax.ShapeDtypeStruct((PLANE *...  174 us
    pallas_call x1, Pallas kernels, tile_product(): pl.pallas_call(tile_kernel, out_shape=jax.ShapeDtypeStruct((blocks, side,...  11.8 us
    pallas_call x1, Pallas kernels, feat_sum(): pl.pallas_call(feat_sum_kernel, out_shape=jax.ShapeDtypeStruct(share.shap...  5.36 us

profile of v7, /device:TPU:1, one launch (start us, length us, event | category | flops | bytes accessed | tf_op | source)
XLA Modules:
  0.0 193.1 jit_solution(6991875031791245777)
XLA Ops:
  0.0 173.8 %shard_map.55 = (f32[80,16,256]{2,1,0:T(8,128)S(1)}, f32[80,16,256]{2,1,0:T(8,128)S(1)}, f32[80,16,256]{2,1,0:T(8,128)S(1)}, f32[80,16,256]{2,1,0:T(8,128)S(1)},...) custom-call(s32[1,128]{1,0:T(1,128)} %bitcast.20, ...), custom_call_target="tpu_custom_call" | custom-call | tf_op jit(solution)/shard_map/pallas_call | solution.py:383
  173.9 11.8 %shard_map.56 = f32[16,128,256]{2,1,0:T(8,128)S(1)} custom-call(s32[2,128]{1,0:T(2,128)S(1)} %get-tuple-element.23.plan, f32[128,128,128]{2,1,0:T(8,128)S(1)} %get-tuple-element.24.tiles, f32[80,16,256]{2,1,0:T(8,128)S(1)} %get-tuple-element.25.rest_0_, f32[80,16,256]{2,1,0:T(8,128)S(1)} %get-tuple-element.26.rest_1_, ...), custom_call_target="tpu_custom_call" | custom-call | tf_op jit(solution)/shard_map/pallas_call | solution.py:50
  185.7 0.0 copy-start
  185.7 0.3 multiply_reduce_fusion.share
  186.0 5.4 %shard_map.57 = f32[16,128]{1,0:T(8,128)S(1)} custom-call(f32[16,128]{1,0:T(8,128)S(1)} %multiply_reduce_fusion.share), custom_call_target="tpu_custom_call" | custom-call | tf_op jit(solution)/shard_map/pallas_call | solution.py:443
  191.4 0.0 copy-done
  191.4 1.7 multiply_multiply_fusion
  (1 shorter events, 0.0 us)
Async XLA Ops:
  185.7 5.7 %copy-start = (f32[256]{0:T(256)S(1)}, f32[256]{0:T(256)}, u32[]{:S(2)}) copy-start(f32[256]{0:T(256)} %param.6) | copy-start | bytes 3076

commit v8 on v7

--- a/solution.py
+++ b/solution.py
@@ -9,7 +9,7 @@
 
 HEAVY = 3
 GROUP = 16
-TOGETHER = 4
+TOGETHER = 8
 
 
 def halves(value):
@@ -23,24 +23,39 @@
     total, light = tiles.shape[0], panel[0].shape[0]
     out[...] = jnp.zeros_like(out)
 
-    def product(t):
-        slot = plan[0, t]
-        is_light, i, j = slot < light, jnp.minimum(slot, light - 1), jnp.maximum(slot - light, 0)
-        x = jnp.concatenate([jnp.where(is_light, panel[k][i], heavy[k][j]) for k in range(PARTS)], axis=0)
-        x_hi, x_lo = halves(jnp.maximum(x, 0.0))
-        a_hi, a_lo = halves(tiles[t])
-        return jnp.dot(
-            jnp.concatenate([a_hi, a_lo], axis=1),
-            jnp.concatenate([x_hi, x_hi], axis=0),
-            preferred_element_type=jnp.float32,
-        ) + jnp.dot(a_hi, x_lo, preferred_element_type=jnp.float32)
-
-    @pl.loop(0, total // TOGETHER)
-    def _(step):
-        ts = [step * TOGETHER + u for u in range(TOGETHER)]
-        products = [product(t) for t in ts]
-        for t, prod in zip(ts, products):
-            out[plan[1, t]] += prod
+    def product(p, source):
+        x_hi, x_lo = halves(jnp.maximum(source(plan[0, p]), 0.0))
+        a = tiles[plan[2, p]]
+        return jnp.dot(a, jnp.concatenate([x_hi, x_hi], axis=0), preferred_element_type=jnp.float32) + jnp.dot(
+            a[:, : a.shape[1] // 2], x_lo, preferred_element_type=jnp.float32
+        )
+
+    def join(parts):
+        return jnp.concatenate(list(parts), axis=0)
+
+    def from_panel(slot):
+        return join(panel[k][slot] for k in range(PARTS))
+
+    def from_heavy(slot):
+        return join(heavy[k][slot - light] for k in range(PARTS))
+
+    def from_either(slot):
+        i, j = jnp.minimum(slot, light - 1), jnp.maximum(slot - light, 0)
+        return join(jnp.where(slot < light, panel[k][i], heavy[k][j]) for k in range(PARTS))
+
+    def run(first, last, source):
+        @pl.loop(first, last)
+        def _(step):
+            ps = [step * TOGETHER + u for u in range(TOGETHER)]
+            products = [product(p, source) for p in ps]
+            for p, prod in zip(ps, products):
+                out[plan[1, p]] += prod
+
+    low = lax.div(plan[3, 0], TOGETHER)
+    high = lax.div(plan[3, 0] + TOGETHER - 1, TOGETHER)
+    run(0, low, from_panel)
+    run(low, high, from_either)
+    run(high, total // TOGETHER, from_heavy)
 
 
 def tile_product(plan, tiles, panel, heavy):
@@ -104,7 +119,13 @@
     side = counts.shape[1]
     ends = total_of(j[:side, :side] <= i[:side, :side], jnp.broadcast_to(counts, (side, side)), 1)
     row = total_of(ends <= j[:side], 1, 0)
-    return request, slot, row
+    turned_slot, turned_row = [jnp.broadcast_to(v, (lanes, lanes)).T for v in (slot, row)]
+    heavy_tile = slot >= devices + blocks
+    light_tiles = total_of(slot < devices + blocks, 1, 1)
+    place = total_of(((turned_slot >= devices + blocks) == heavy_tile) & (i < j), 1, 0) + jnp.where(heavy_tile, light_tiles, 0)
+    here = jnp.broadcast_to(place, (lanes, lanes)).T == j
+    ordered = [total_of(here, v, 0) for v in (turned_slot, turned_row, i)]
+    return request, ordered + [jnp.broadcast_to(light_tiles, (1, lanes))]
 
 
 def exchange_kernel(cols, counts, features, tiles, *rest):
@@ -113,7 +134,7 @@
     names = ("own", "up1", "down1", "up2", "down2", "up3s", "down3s", "up3", "down3", "far", "picked")
     bufs = {n: scratch[i * PARTS : (i + 1) * PARTS] for i, n in enumerate(names)}
     own, up1, down1, up2, down2, up3s, down3s, up3, down3, far, picked = (bufs[n] for n in names)
-    (rows_buf, table, load_sem, zs, zr, xs, xr, gs, gr, out_sem, ps, pr, table_sem, tile_sem, cols_buf, counts_buf, small_sem) = scratch[len(names) * PARTS :]
+    (rows_buf, table, load_sem, zs, zr, xs, xr, gs, gr, out_sem, ps, pr, table_sem, staged, tile_sem, cols_buf, counts_buf, small_sem) = scratch[len(names) * PARTS :]
     me = lax.axis_index("rows")
     z, q = me // PLANE, lax.rem(me, PLANE)
     x, c = q // 2, lax.rem(q, 2)
@@ -140,8 +161,24 @@
     )
     for copy in small_loads:
         copy.start()
-    tile_load = pltpu.make_async_copy(tiles, tiles_out, tile_sem)
-    tile_load.start()
+    lot = staged.shape[1]
+
+    def tile_load(n):
+        return pltpu.make_async_copy(tiles.at[pl.ds(n * lot, lot)], staged.at[n % 2], tile_sem.at[n % 2])
+
+    def split_tiles(n):
+        tile_load(n).wait()
+
+        @pl.loop(0, lot)
+        def _(i):
+            high, low = halves(staged[n % 2, i])
+            tiles_out[n * lot + i] = jnp.concatenate([high, low], axis=1)
+
+        if (n + 2) * lot < tiles.shape[0]:
+            tile_load(n + 2).start()
+
+    for n in range(2):
+        tile_load(n).start()
     barrier = pltpu.get_barrier_semaphore()
     second_up, second_down = at(2) * PLANE + q, at(-2) * PLANE + q
     for peer in (up, down, second_up, second_down):
@@ -168,8 +205,8 @@
         )[step]
         i = (k * 4 + step) * 2
         return (
-            send(src_up, dst_up, zs.at[i], zr.at[i], up),
-            send(src_down, dst_down, zs.at[i + 1], zr.at[i + 1], down),
+            send(src_up, dst_up, zs.at[k], zr.at[i], up),
+            send(src_down, dst_down, zs.at[PARTS + k], zr.at[i + 1], down),
         )
 
     def z_start(k, step):
@@ -198,9 +235,9 @@
     def share_plan():
         for copy in small_loads:
             copy.wait()
-        request, slot, row = plan_rows(me, cols_buf[...], counts_buf[...], own[0].shape[0])
-        plan_out[0:1] = slot
-        plan_out[1:2] = row
+        request, plan = plan_rows(me, cols_buf[...], counts_buf[...], own[0].shape[0])
+        for i, line in enumerate(plan):
+            plan_out[i : i + 1] = line
         rows_buf[me] = request
 
         @pl.loop(1, PLANE)
@@ -255,7 +292,7 @@
 
     def pieces_copy(k, i, qq, part, peer):
         piece = gathered[k].at[qq, part]
-        return send(piece, piece, gs.at[k * 15 + i], gr.at[k * 15 + i], peer)
+        return send(piece, piece, gs.at[k], gr.at[k * 15 + i], peer)
 
     def to_partner(k):
         return pieces_copy(k, 14, q, 1 - even, partner)
@@ -278,6 +315,16 @@
     def z_first(k):
         load(k).wait()
         z_start(k, 0)
+
+    def all_blocks(k, count, sem):
+        whole = arrived[k].at[pl.ds(0, count)]
+        pltpu.make_async_copy(whole, whole, sem).wait()
+
+    def plan_sent():
+        most = rows_buf.at[pl.ds(0, PLANE - 1)]
+        pltpu.make_async_copy(most, most, ps.at[0]).wait()
+        for i in range(4):
+            rows_copy(i).wait_send()
 
     def stage(k, s):
         if s == 0:
@@ -323,13 +370,17 @@
             z_wait(k, 3)
             x_pass(k, 7, lambda reader: far[k].at[lax.rem(reader, 2), reader // 2])
         elif s == 5:
-            everything = arrived[k].at[pl.ds(0, (PLANE - 1) * PLANES)]
-            pltpu.make_async_copy(everything, everything, xr.at[k]).wait()
+            all_blocks(k, (PLANE - 1) * PLANES, xr.at[k])
             keep_own(k).wait()
             for i in range(HEAVY):
                 gathered[k][q, 1 - even, i] = arrived[k][table[me, 0, PLANES * PLANE + i]]
             for copy in [to_partner(k)] + over_x(k, 0) + to_core(k, 0)[:1]:
                 copy.start()
+            if k == 0:
+                plan_sent()
+            for sem in (zs.at[k], zs.at[PARTS + k]):
+                all_blocks(k, 2 * own[k].shape[0] + PLANE + 8, sem)
+            all_blocks(k, (PLANE - 1) * PLANES, xs.at[k])
         elif s == 6:
             to_partner(k).wait_recv()
             for copy in over_x(k, 1) + to_core(k, 1)[:1]:
@@ -351,25 +402,15 @@
         elif s == 9:
             for copy in to_core(k, 0) + to_core(k, 1):
                 copy.wait_recv()
+            all_blocks(k, 15 * HEAVY, gs.at[k])
 
     for t in range(PARTS + 9):
         for s, lag in ORDER:
             if 0 <= t - lag < PARTS:
                 stage(t - lag, s)
-
-    tile_load.wait()
-    most = rows_buf.at[pl.ds(0, PLANE - 1)]
-    pltpu.make_async_copy(most, most, ps.at[0]).wait()
-    for i in range(4):
-        rows_copy(i).wait_send()
-    for k in range(PARTS):
-        for step in range(4):
-            for copy in z_copies(k, step):
-                copy.wait_send()
-        everything = arrived[k].at[pl.ds(0, (PLANE - 1) * PLANES)]
-        pltpu.make_async_copy(everything, everything, xs.at[k]).wait()
-        for copy in [to_partner(k)] + over_x(k, 0) + over_x(k, 1) + [across(k, 0), across(k, 1)] + to_core(k, 0) + to_core(k, 1):
-            copy.wait_send()
+        for n in (2 * t, 2 * t + 1):
+            if n * lot < tiles.shape[0]:
+                split_tiles(n)
 
 
 def exchange(cols, counts, own, tiles):
@@ -384,7 +425,8 @@
         exchange_kernel,
         out_shape=[jax.ShapeDtypeStruct((PLANE * PLANES + blocks, rows, feat), jnp.float32)] * PARTS
         + [jax.ShapeDtypeStruct((PLANE, 2, HEAVY, rows, feat), jnp.float32)] * PARTS
-        + [jax.ShapeDtypeStruct((2, cols.shape[1]), jnp.int32), jax.ShapeDtypeStruct(tiles.shape, jnp.float32)],
+        + [jax.ShapeDtypeStruct((4, cols.shape[1]), jnp.int32)]
+        + [jax.ShapeDtypeStruct(tiles.shape[:2] + (2 * tiles.shape[2],), jnp.bfloat16)],
         in_specs=[hbm] * 4,
         out_specs=[vmem] * (2 * PARTS + 2),
         scratch_shapes=bufs
@@ -392,17 +434,18 @@
             pltpu.VMEM((PLANE * PLANES, 1, cols.shape[1]), jnp.int32),
             pltpu.SMEM((PLANE * PLANES, 1, cols.shape[1]), jnp.int32),
             dma((PARTS,)),
-            dma((PARTS * 8,)),
+            dma((PARTS * 2,)),
             dma((PARTS * 8,)),
             dma((PARTS,)),
             dma((PARTS,)),
-            dma((PARTS * 15,)),
+            dma((PARTS,)),
             dma((PARTS * 15,)),
             dma((PARTS,)),
             dma((5,)),
             dma((5,)),
             dma((5,)),
-            dma,
+            pltpu.VMEM((2, 8) + tiles.shape[1:], jnp.float32),
+            dma((2,)),
             pltpu.VMEM(cols.shape, jnp.int32),
             pltpu.VMEM(counts.shape, jnp.int32),
             dma((2,)),

time: 193 us -> 188 us (0.974)
  Pallas kernels: 191 us -> 186 us
    pallas_call x1, Pallas kernels: 11.8 us -> 9 us  [tile_product(): pl.pallas_call(tile_kernel, out_shape=jax.ShapeDtypeStruct((blocks, side,...]
    pallas_call x1, Pallas kernels: 174 us -> 172 us  [exchange(): pl.pallas_call(exchange_kernel, out_shape=[jax.ShapeDtypeStruct((PLANE *...]
where the time goes in v8:
time: 188 us
  Pallas kernels  186 us (99%)
  other arithmetic  2.02 us (1%)
    pallas_call x1, Pallas kernels, exchange(): pl.pallas_call(exchange_kernel, out_shape=[jax.ShapeDtypeStruct((PLANE *...  172 us
    pallas_call x1, Pallas kernels, tile_product(): pl.pallas_call(tile_kernel, out_shape=jax.ShapeDtypeStruct((blocks, side,...  9 us
    pallas_call x1, Pallas kernels, feat_sum(): pl.pallas_call(feat_sum_kernel, out_shape=jax.ShapeDtypeStruct(share.shap...  5.28 us

profile of v8, /device:TPU:1, one launch (start us, length us, event | category | flops | bytes accessed | tf_op | source)
XLA Modules:
  0.0 188.1 jit_solution(2778308136055658882)
XLA Ops:
  0.0 171.7 %shard_map.55 = (f32[80,16,256]{2,1,0:T(8,128)S(1)}, f32[80,16,256]{2,1,0:T(8,128)S(1)}, f32[80,16,256]{2,1,0:T(8,128)S(1)}, f32[80,16,256]{2,1,0:T(8,128)S(1)},...) custom-call(s32[1,128]{1,0:T(1,128)} %bitcast.20, ...), custom_call_target="tpu_custom_call" | custom-call | tf_op jit(solution)/shard_map/pallas_call | solution.py:424
  171.8 9.0 %shard_map.56 = f32[16,128,256]{2,1,0:T(8,128)S(1)} custom-call(s32[4,128]{1,0:T(4,128)S(1)} %get-tuple-element.23.plan, bf16[128,128,256]{2,1,0:T(8,128)(2,1)S(1)} %get-tuple-element.24.tiles, f32[80,16,256]{2,1,0:T(8,128)S(1)} %get-tuple-element.25.rest_0_, f32[80,16,256]{2,1,0:T(8,128)S(1)} %get-tuple-element.26.rest_1_, ...), custom_call_target="tpu_custom_call" | custom-call | tf_op jit(solution)/shard_map/pallas_call | solution.py:65
  180.8 0.0 copy-start
  180.8 0.3 multiply_reduce_fusion.share
  181.1 5.3 %shard_map.57 = f32[16,128]{1,0:T(8,128)S(1)} custom-call(f32[16,128]{1,0:T(8,128)S(1)} %multiply_reduce_fusion.share), custom_call_target="tpu_custom_call" | custom-call | tf_op jit(solution)/shard_map/pallas_call | solution.py:486
  186.4 0.0 copy-done
  186.4 1.7 multiply_multiply_fusion
  (1 shorter events, 0.0 us)
Async XLA Ops:
  180.8 5.7 %copy-start = (f32[256]{0:T(256)S(1)}, f32[256]{0:T(256)}, u32[]{:S(2)}) copy-start(f32[256]{0:T(256)} %param.6) | copy-start | bytes 3076

commit v9 on v8

--- a/solution.py
+++ b/solution.py
@@ -9,7 +9,7 @@
 
 HEAVY = 3
 GROUP = 16
-TOGETHER = 8
+TOGETHER = 16
 
 
 def halves(value):
@@ -74,6 +74,7 @@
 PARTS = 8
 PLANE = 8
 PLANES = 8
+STRAIGHT = 1
 ORDER = tuple((stage, stage) for stage in range(10))
 MESH = pl.DeviceIdType.MESH
 
@@ -145,9 +146,9 @@
 
     up, down = at(1) * PLANE + q, at(-1) * PLANE + q
     even = 1 - lax.rem(z, 2)
-    partner = (z + 2 * even - 1) * PLANE + q
     right = z * PLANE + lax.rem(x + 1, 4) * 2 + c
     left = z * PLANE + lax.rem(x + 3, 4) * 2 + c
+    opposite = z * PLANE + lax.rem(x + 2, 4) * 2 + c
     other = z * PLANE + x * 2 + 1 - c
 
     def load(k):
@@ -295,14 +296,20 @@
         return send(piece, piece, gs.at[k], gr.at[k * 15 + i], peer)
 
     def to_partner(k):
-        return pieces_copy(k, 14, q, 1 - even, partner)
+        return pieces_copy(k, 14, q, 1 - even, jnp.where(even == k % 2, up, down))
 
     def over_x(k, p):
         part = even if p else 1 - even
         return [pieces_copy(k, p * 7 + i, q, part, peer) for i, peer in enumerate((right, left))]
 
+    def direct(k):
+        return k >= PARTS - STRAIGHT
+
     def across(k, p):
-        return pieces_copy(k, p * 7 + 2, q_of(1 if p else -1), even if p else 1 - even, left if p else right)
+        part, i = even if p else 1 - even, p * 7 + 2
+        if direct(k):
+            return pieces_copy(k, i, q, part, opposite)
+        return pieces_copy(k, i, q_of(1 if p else -1), part, left if p else right)
 
     def to_core(k, p):
         part = even if p else 1 - even
@@ -374,7 +381,7 @@
             keep_own(k).wait()
             for i in range(HEAVY):
                 gathered[k][q, 1 - even, i] = arrived[k][table[me, 0, PLANES * PLANE + i]]
-            for copy in [to_partner(k)] + over_x(k, 0) + to_core(k, 0)[:1]:
+            for copy in [to_partner(k)] + over_x(k, 0) + [across(k, 0)] * direct(k) + to_core(k, 0)[:1]:
                 copy.start()
             if k == 0:
                 plan_sent()
@@ -383,16 +390,16 @@
             all_blocks(k, (PLANE - 1) * PLANES, xs.at[k])
         elif s == 6:
             to_partner(k).wait_recv()
-            for copy in over_x(k, 1) + to_core(k, 1)[:1]:
+            for copy in over_x(k, 1) + [across(k, 1)] * direct(k) + to_core(k, 1)[:1]:
                 copy.start()
             for came in over_x(k, 0):
                 came.wait_recv()
-            for copy in [across(k, 0)] + to_core(k, 0)[1:3]:
+            for copy in [across(k, 0)] * (not direct(k)) + to_core(k, 0)[1:3]:
                 copy.start()
         elif s == 7:
             for came in over_x(k, 1):
                 came.wait_recv()
-            for copy in [across(k, 1)] + to_core(k, 1)[1:3]:
+            for copy in [across(k, 1)] * (not direct(k)) + to_core(k, 1)[1:3]:
                 copy.start()
             across(k, 0).wait_recv()
             to_core(k, 0)[3].start()

time: 188 us -> 187 us (level)
  no operation moved by 1% of the time
where the time goes in v9:
time: 187 us
  Pallas kernels  185 us (99%)
  other arithmetic  2.02 us (1%)
    pallas_call x1, Pallas kernels, exchange(): pl.pallas_call(exchange_kernel, out_shape=[jax.ShapeDtypeStruct((PLANE *...  171 us
    pallas_call x1, Pallas kernels, tile_product(): pl.pallas_call(tile_kernel, out_shape=jax.ShapeDtypeStruct((blocks, side,...  7.91 us
    pallas_call x1, Pallas kernels, feat_sum(): pl.pallas_call(feat_sum_kernel, out_shape=jax.ShapeDtypeStruct(share.shap...  5.27 us

profile of v9, /device:TPU:1, one launch (start us, length us, event | category | flops | bytes accessed | tf_op | source)
XLA Modules:
  0.0 186.7 jit_solution(8449077955912584531)
XLA Ops:
  0.0 171.5 %shard_map.55 = (f32[80,16,256]{2,1,0:T(8,128)S(1)}, f32[80,16,256]{2,1,0:T(8,128)S(1)}, f32[80,16,256]{2,1,0:T(8,128)S(1)}, f32[80,16,256]{2,1,0:T(8,128)S(1)},...) custom-call(s32[1,128]{1,0:T(1,128)} %bitcast.20, ...), custom_call_target="tpu_custom_call" | custom-call | tf_op jit(solution)/shard_map/pallas_call | solution.py:431
  171.5 7.9 %shard_map.56 = f32[16,128,256]{2,1,0:T(8,128)S(1)} custom-call(s32[4,128]{1,0:T(4,128)S(1)} %get-tuple-element.23.plan, bf16[128,128,256]{2,1,0:T(8,128)(2,1)S(1)} %get-tuple-element.24.tiles, f32[80,16,256]{2,1,0:T(8,128)S(1)} %get-tuple-element.25.rest_0_, f32[80,16,256]{2,1,0:T(8,128)S(1)} %get-tuple-element.26.rest_1_, ...), custom_call_target="tpu_custom_call" | custom-call | tf_op jit(solution)/shard_map/pallas_call | solution.py:65
  179.4 0.0 copy-start
  179.4 0.3 multiply_reduce_fusion.share
  179.7 5.3 %shard_map.57 = f32[16,128]{1,0:T(8,128)S(1)} custom-call(f32[16,128]{1,0:T(8,128)S(1)} %multiply_reduce_fusion.share), custom_call_target="tpu_custom_call" | custom-call | tf_op jit(solution)/shard_map/pallas_call | solution.py:493
  185.0 0.0 copy-done
  185.0 1.7 multiply_multiply_fusion
  (1 shorter events, 0.0 us)
Async XLA Ops:
  179.4 5.7 %copy-start = (f32[256]{0:T(256)S(1)}, f32[256]{0:T(256)}, u32[]{:S(2)}) copy-start(f32[256]{0:T(256)} %param.6) | copy-start | bytes 3076

commit v10 on v9

--- a/solution.py
+++ b/solution.py
@@ -385,9 +385,6 @@
                 copy.start()
             if k == 0:
                 plan_sent()
-            for sem in (zs.at[k], zs.at[PARTS + k]):
-                all_blocks(k, 2 * own[k].shape[0] + PLANE + 8, sem)
-            all_blocks(k, (PLANE - 1) * PLANES, xs.at[k])
         elif s == 6:
             to_partner(k).wait_recv()
             for copy in over_x(k, 1) + [across(k, 1)] * direct(k) + to_core(k, 1)[:1]:
@@ -409,6 +406,9 @@
         elif s == 9:
             for copy in to_core(k, 0) + to_core(k, 1):
                 copy.wait_recv()
+            for sem in (zs.at[k], zs.at[PARTS + k]):
+                all_blocks(k, 2 * own[k].shape[0] + PLANE + 8, sem)
+            all_blocks(k, (PLANE - 1) * PLANES, xs.at[k])
             all_blocks(k, 15 * HEAVY, gs.at[k])
 
     for t in range(PARTS + 9):

time: 187 us -> 187 us (level)
  no operation moved by 1% of the time
where the time goes in v10:
time: 187 us
  Pallas kernels  185 us (99%)
  other arithmetic  2.02 us (1%)
    pallas_call x1, Pallas kernels, exchange(): pl.pallas_call(exchange_kernel, out_shape=[jax.ShapeDtypeStruct((PLANE *...  171 us
    pallas_call x1, Pallas kernels, tile_product(): pl.pallas_call(tile_kernel, out_shape=jax.ShapeDtypeStruct((blocks, side,...  7.88 us
    pallas_call x1, Pallas kernels, feat_sum(): pl.pallas_call(feat_sum_kernel, out_shape=jax.ShapeDtypeStruct(share.shap...  5.27 us

profile of v10, /device:TPU:1, one launch (start us, length us, event | category | flops | bytes accessed | tf_op | source)
XLA Modules:
  0.0 186.7 jit_solution(9266641743688343134)
XLA Ops:
  0.0 171.5 %shard_map.55 = (f32[80,16,256]{2,1,0:T(8,128)S(1)}, f32[80,16,256]{2,1,0:T(8,128)S(1)}, f32[80,16,256]{2,1,0:T(8,128)S(1)}, f32[80,16,256]{2,1,0:T(8,128)S(1)},...) custom-call(s32[1,128]{1,0:T(1,128)} %bitcast.20, ...), custom_call_target="tpu_custom_call" | custom-call | tf_op jit(solution)/shard_map/pallas_call | solution.py:431
  171.5 7.9 %shard_map.56 = f32[16,128,256]{2,1,0:T(8,128)S(1)} custom-call(s32[4,128]{1,0:T(4,128)S(1)} %get-tuple-element.23.plan, bf16[128,128,256]{2,1,0:T(8,128)(2,1)S(1)} %get-tuple-element.24.tiles, f32[80,16,256]{2,1,0:T(8,128)S(1)} %get-tuple-element.25.rest_0_, f32[80,16,256]{2,1,0:T(8,128)S(1)} %get-tuple-element.26.rest_1_, ...), custom_call_target="tpu_custom_call" | custom-call | tf_op jit(solution)/shard_map/pallas_call | solution.py:65
  179.4 0.0 copy-start
  179.4 0.3 multiply_reduce_fusion.share
  179.7 5.3 %shard_map.57 = f32[16,128]{1,0:T(8,128)S(1)} custom-call(f32[16,128]{1,0:T(8,128)S(1)} %multiply_reduce_fusion.share), custom_call_target="tpu_custom_call" | custom-call | tf_op jit(solution)/shard_map/pallas_call | solution.py:493
  185.0 0.0 copy-done
  185.0 1.7 multiply_multiply_fusion
  (1 shorter events, 0.0 us)
Async XLA Ops:
  179.4 5.7 %copy-start = (f32[256]{0:T(256)S(1)}, f32[256]{0:T(256)}, u32[]{:S(2)}) copy-start(f32[256]{0:T(256)} %param.6) | copy-start | bytes 3076
